TPU v7x, 256 devices: a whole 4x4x8 slice. The times are simulated.
256 devices in a mesh: lon: 32 (over z, x_lo, core), mem: 8 (over y, x_hi).
Axes of the slice: x: 4 (x_hi: 2, x_lo: 2; x = x_hi * 2 + x_lo), y: 4, z: 8, core: 2. Of those that a mesh axis runs over, the one named last changes fastest.
Arguments:
- assimilated_snapshot: bfloat16 [8, 1440, 128], P(None, 'lon'), may hold values from -6 to 6
- stochastic_displacement: bfloat16 [8, 8, 1440, 128], P('mem', None, 'lon'), may hold values from -3 to 3
- outcome_cotangent_vector: bfloat16 [8, 8, 1440, 128], P('mem', None, 'lon'), may hold values from -6 to 6
- spatial_window_coefficients: bfloat16 [3, 1152, 128], replicated, may hold values from -0.1875 to 0.1875
- mixer_entry_projection: bfloat16 [3, 128, 512], replicated, may hold values from -0.5 to 0.5
- mixer_exit_projection: bfloat16 [3, 512, 128], replicated, may hold values from -0.25 to 0.25
- spacing_per_tier: int32 [3], replicated, may hold values from 1 to 144, as said below
Outputs:
- trajectory_outcomes: bfloat16 [8, 8, 1440, 128], P('mem', None, 'lon')
- starting_point_partials: bfloat16 [8, 8, 1440, 128], P('mem', None, 'lon')
- filter_weight_derivative: float32 [3, 1152, 128], P(None, 'mem')
Inputs may be any that keep to these rules, and one draw needn't show every extreme that they name: `spacing_per_tier`: dilations count longitude columns; in every draw some layer has dilation 144.
All inputs are finite; a program needn't handle non-finite values.
Results may differ from a plain program's by a relative error of at most 0.028.
Values may be sent and summed in bfloat16 or wider, within the bound.
No kernel may reach another device: no remote copies, remote signals or barrier semaphores. Data moves between devices by JAX's collectives and lax.ppermute only.
A program may use at most 64 MiB of HBM per device.

v0:
```python
import functools
import math

import jax
import jax.numpy as jnp
from jax import lax
from jax.experimental import pallas as pl
from jax.experimental.pallas import tpu as pltpu
from jax.sharding import Mesh
from jax.sharding import PartitionSpec as P

MAXD = 144
LAYERS = 3
PLANE = ("xl", "core")
LON = ("z",) + PLANE
F32 = jnp.float32
BF16 = jnp.bfloat16


def passed_along(block, axis, distance):
    devices = range(lax.axis_size(axis))
    route = [((i - distance) % len(devices), i) for i in devices]
    return lax.ppermute(block, axis, route)


def slope(values):
    sig = jax.nn.sigmoid(values)
    return sig * (1.0 + values * (1.0 - sig))


def matmul(a, b, dims=((1,), (0,))):
    return lax.dot_general(a, b, (dims, ((), ())), preferred_element_type=F32)


def exchange(field, near, ncols):
    hops = (MAXD + ncols - 1) // ncols

    def within(near):
        def fetch(field):
            return (
                passed_along(field, LON, near + 1),
                passed_along(field, LON, near) if near else field,
                passed_along(field, LON, -near) if near else field,
                passed_along(field, LON, -near - 1),
            )

        return fetch

    return lax.switch(near, [within(k) for k in range(hops)], field)


class Sizes:
    def __init__(self, rows, ncols, chans, hidden):
        self.rows, self.ncols, self.chans, self.hidden = rows, ncols, chans, hidden
        self.pitch = (ncols + 15) // 16 * 16
        self.cells = rows * self.pitch


def fill_shifted(size, rest, parts, scratches):
    far_lower, near_lower, own, near_upper, far_upper = parts
    pitch, ncols = size.pitch, size.ncols
    shape = (pitch, 2 * pitch)
    col = lax.broadcasted_iota(jnp.int32, shape, 0)
    src = lax.broadcasted_iota(jnp.int32, shape, 1)
    live = (col < ncols) & (src < 2 * pitch)
    at = jnp.where(src < pitch, src, src - pitch + ncols)
    live = live & ((src < ncols) | ((src >= pitch) & (src < pitch + ncols)))
    picks = []
    for begin in (ncols - rest, rest):
        picks.append(jnp.where(live & (at == col + begin), 1.0, 0.0).astype(BF16))
    zero = jnp.zeros((pitch, size.chans), BF16)
    for scratch in scratches:
        scratch[pl.ds(0, pitch), :] = zero
        scratch[pl.ds(pitch + size.cells, pitch), :] = zero
    scratches[1][pl.ds(pitch, size.cells), :] = own
    for pick, first, second, scratch in (
        (picks[0], far_lower, near_lower, scratches[0]),
        (picks[1], near_upper, far_upper, scratches[2]),
    ):
        for row in range(size.rows):
            span = pl.ds(row * pitch, pitch)
            pair = jnp.concatenate([first[span, :], second[span, :]], axis=0)
            scratch[pl.ds(pitch + row * pitch, pitch), :] = matmul(pick, pair).astype(BF16)


def taps_of(size, scratches):
    pieces = []
    for off in range(3):
        for scratch in scratches:
            pieces.append(scratch[pl.ds(off * size.pitch, size.cells), :])
    return jnp.concatenate(pieces, axis=1)


def valid_cells(size):
    col = lax.broadcasted_iota(jnp.int32, (size.rows, size.pitch, 1), 1)
    return (col < size.ncols).reshape(size.cells, 1)


def padded_into(size, scratch, values):
    scratch[...] = jnp.zeros(scratch.shape, scratch.dtype)
    for row in range(size.rows):
        scratch[pl.ds(row * size.pitch, size.ncols), :] = values(row).astype(scratch.dtype)


def unpadded_into(size, out, values):
    for row in range(size.rows):
        out[row] = values[row * size.pitch : row * size.pitch + size.ncols, :].astype(out.dtype)


def silu(values):
    return values * jax.nn.sigmoid(values)


def begin_body(size, a_ref, b_ref, field, *unwritten):
    padded_into(size, field, lambda row: a_ref[row].astype(F32) + b_ref[row].astype(F32))


def stage_body(
    size, stage_ref, spacing_ref, fl, nl, nu, fu, entry, leave, cot, conv, field_in, grad_in, *refs
):
    field, grad_out, hidden, mixed, pre_conv, lower, upper, terms, outcome, first = refs[8:18]
    left, middle, right, back, kernel, own, narrow, pre, before, after, found, block, sems = refs[18:]
    stage = stage_ref[0]
    forward = stage < LAYERS
    turn = stage == LAYERS - 1
    final = stage == 2 * LAYERS - 1
    layer = jnp.where(forward, stage, 2 * LAYERS - 1 - stage)
    at = jnp.where(forward, stage, jnp.maximum(2 * LAYERS - 2 - stage, 0))
    kept = jnp.minimum(at, LAYERS - 2)
    inner = pl.ds(size.pitch, size.cells)
    pairs = (
        (hidden, own.at[inner]), (mixed, narrow), (pre_conv, pre), (lower, before), (upper, after)
    )
    weights = pltpu.make_async_copy(conv.at[layer], kernel, sems.at[0])
    loads = [
        pltpu.make_async_copy(there.at[kept], here, sems.at[1 + i])
        for i, (there, here) in enumerate(pairs)
    ]
    saves = [
        pltpu.make_async_copy(here, there.at[kept], sems.at[1 + i])
        for i, (there, here) in enumerate(pairs)
    ]
    weights.start()

    @pl.when(~forward & ~final)
    def _():
        for copy in loads:
            copy.start()

    spacing = spacing_ref[layer]
    near = sum((spacing > hop * size.ncols).astype(jnp.int32) for hop in range(1, size.hops))
    shifted = (left, middle, right)
    fill_shifted(size, spacing - near * size.ncols, (fl, nl, field_in[...], nu, fu), shifted)
    weights.wait()

    @pl.when(forward)
    def _():
        mine = middle[inner, :]
        taps = taps_of(size, shifted)
        before[...] = left[...]
        after[...] = right[...]
        own[...] = middle[...]
        value = matmul(taps, kernel[...])
        total = mine.astype(F32) + silu(value)
        small = total.astype(BF16)
        pre[...] = value
        narrow[...] = small
        act = silu(matmul(small, entry[at])).astype(BF16)
        total = total + matmul(act, leave[at])

        @pl.when(~turn)
        def _():
            for copy in saves:
                copy.start()
            field[...] = jnp.where(valid_cells(size), total, 0.0).astype(BF16)
            for copy in saves:
                copy.wait()

        @pl.when(turn)
        def _():
            unpadded_into(size, block, total)
            copy = pltpu.make_async_copy(block, outcome, sems.at[6])
            copy.start()
            padded_into(size, back, lambda row: cot[row])
            copy.wait()

    @pl.when(~forward)
    def _():
        chans = size.chans
        turned = jnp.concatenate(
            [kernel[pl.ds((8 - tap) * chans, chans), :] for tap in range(9)], axis=1
        )
        total = grad_in[...] + matmul(taps_of(size, shifted), turned, ((1,), (1,)))
        back[...] = jnp.where(valid_cells(size), total, 0.0).astype(BF16)

        @pl.when(final)
        def _():
            unpadded_into(size, block, back)
            copy = pltpu.make_async_copy(block, first, sems.at[6])
            copy.start()
            copy.wait()

        @pl.when(~final)
        def _():
            own[pl.ds(0, size.pitch), :] = jnp.zeros((size.pitch, chans), BF16)
            own[pl.ds(size.pitch + size.cells, size.pitch), :] = jnp.zeros(
                (size.pitch, chans), BF16
            )
            for copy in loads:
                copy.wait()

    @pl.when((stage >= LAYERS - 1) & ~final)
    def _():
        came = back[...]
        pre_mlp = matmul(narrow[...], entry[at])
        grad_pre = (matmul(came, leave[at], ((1,), (1,))) * slope(pre_mlp)).astype(BF16)
        grad = came.astype(F32) + matmul(grad_pre, entry[at], ((1,), (1,)))
        grad_out[...] = grad
        grad_conv = (grad * slope(pre[...])).astype(BF16)
        field[...] = grad_conv
        taps = taps_of(size, (before, own, after))
        values = matmul(grad_conv, taps, ((0,), (0,)))
        chans = size.chans
        for tap in range(9):
            found[pl.ds(tap * chans, chans), :] = values[:, tap * chans : (tap + 1) * chans].T.astype(
                BF16
            )
        count = 9 * chans // size.members
        copies = []
        for member in range(size.members):
            to = pl.multiple_of(member * size.share + at * count, 16)
            copies.append(
                pltpu.make_async_copy(
                    found.at[pl.ds(member * count, count)],
                    terms.at[pl.ds(to, count)],
                    sems.at[7 + member],
                )
            )
        for copy in copies:
            copy.start()
        for copy in copies:
            copy.wait()


VMEM_SPEC = pl.BlockSpec(memory_space=pltpu.VMEM)
SMEM_SPEC = pl.BlockSpec(memory_space=pltpu.SMEM)
ANY_SPEC = pl.BlockSpec(memory_space=pl.ANY)


def total_over_all(size, terms):
    places = size.members * 4
    each = terms.shape[0] // places
    terms = lax.all_to_all(terms.reshape(places, each, size.chans), ("mem",) + PLANE, 0, 0)
    mine = jnp.sum(terms.astype(F32), axis=0).astype(BF16)
    planes = range(lax.axis_size("z"))
    came = [mine.astype(F32)]
    for flip in planes[1:]:
        came.append(lax.ppermute(mine, "z", [(i ^ flip, i) for i in planes]).astype(F32))
    while len(came) > 1:
        came = [a + b for a, b in zip(came[::2], came[1::2])]
    full = lax.all_gather(came[0].astype(BF16), PLANE).reshape(size.share, size.chans)
    own = 9 * size.chans // size.members
    return full[: LAYERS * own].reshape(LAYERS, own, size.chans).astype(F32)


def per_device(
    assimilated_snapshot,
    stochastic_displacement,
    outcome_cotangent_vector,
    spatial_window_coefficients,
    mixer_entry_projection,
    mixer_exit_projection,
    spacing_per_tier,
):
    rows, ncols, chans = assimilated_snapshot.shape
    size = Sizes(rows, ncols, chans, mixer_entry_projection.shape[2])
    size.hops = (MAXD + ncols - 1) // ncols
    size.members = lax.axis_size("mem")
    size.share = (LAYERS * 9 * chans // size.members + 63) // 64 * 64
    tall = (size.cells + 2 * size.pitch, chans)
    cells = (size.cells, chans)

    def array(*shape, dtype=BF16):
        return jax.ShapeDtypeStruct(shape, dtype)

    kinds = [
        array(*cells),
        array(*cells, dtype=F32),
        array(LAYERS - 1, *cells),
        array(LAYERS - 1, *cells),
        array(LAYERS - 1, *cells, dtype=F32),
        array(LAYERS - 1, *tall),
        array(LAYERS - 1, *tall),
        array(size.members * size.share, chans),
        array(rows, ncols, chans),
        array(rows, ncols, chans),
    ]
    held = len(kinds)
    state = pl.pallas_call(
        functools.partial(begin_body, size),
        out_shape=kinds,
        in_specs=[VMEM_SPEC] * 2,
        out_specs=[VMEM_SPEC] + [ANY_SPEC] * (held - 1),
        name="begin",
    )(assimilated_snapshot, stochastic_displacement[0])
    near = sum((spacing_per_tier > hop * ncols).astype(jnp.int32) for hop in range(1, size.hops))
    near = jnp.concatenate([near, near[::-1]])
    state_specs = [VMEM_SPEC] * 2 + [ANY_SPEC] * (held - 2)
    stage_call = pl.pallas_call(
        functools.partial(stage_body, size),
        out_shape=kinds,
        in_specs=[SMEM_SPEC] * 2 + [VMEM_SPEC] * 7 + [ANY_SPEC] + state_specs,
        out_specs=state_specs,
        scratch_shapes=[pltpu.VMEM(tall, BF16)] * 3
        + [
            pltpu.VMEM(cells, BF16),
            pltpu.VMEM((9 * chans, chans), BF16),
            pltpu.VMEM(tall, BF16),
            pltpu.VMEM(cells, BF16),
            pltpu.VMEM(cells, F32),
            pltpu.VMEM(tall, BF16),
            pltpu.VMEM(tall, BF16),
            pltpu.VMEM((9 * chans, chans), BF16),
            pltpu.VMEM((rows, ncols, chans), BF16),
            pltpu.SemaphoreType.DMA((7 + size.members,)),
        ],
        input_output_aliases={10 + i: i for i in range(held)},
        name="stage",
    )

    def step(stage, state):
        blocks = exchange(state[0], near[stage], ncols)
        return tuple(
            stage_call(
                stage.reshape(1),
                spacing_per_tier,
                *blocks,
                mixer_entry_projection,
                mixer_exit_projection,
                outcome_cotangent_vector[0],
                spatial_window_coefficients,
                *state,
            )
        )

    state = lax.fori_loop(0, 2 * LAYERS, step, tuple(state))
    share = total_over_all(size, state[7])
    member_count = size.members * stochastic_displacement.shape[0]
    scale = 1.0 / math.sqrt(member_count * rows * ncols * lax.axis_size(LON))
    return (state[8][None], state[9][None], share * scale)


def solution(mesh):
    fine = Mesh(mesh.devices.reshape(-1, 2, 2, mesh.shape["mem"]), LON + ("mem",))
    placed = (
        P(None, LON, None),
        P("mem", None, LON, None),
        P("mem", None, LON, None),
        P(),
        P(),
        P(),
        P(),
    )
    return jax.shard_map(
        per_device,
        mesh=fine,
        in_specs=placed,
        out_specs=(P("mem", None, LON, None), P("mem", None, LON, None), P(None, "mem", None)),
        check_vma=False,
    )
```

profile of v0, /device:TPU:1, one launch (start us, length us, event | category | flops | bytes accessed | tf_op | source)
XLA Modules:
  0.0 143.9 jit_solution(7105467042358874405)
XLA Ops:
  0.7 1.6 %copy.28 = bf16[1,8,45,128]{3,2,1,0:T(8,128)(2,1)} copy(bf16[1,8,45,128]{3,1,2,0:T(8,128)(2,1)} %param.14) | data formatting | bytes 184320 | tf_op args[1]
  2.3 1.5 %copy.21.a_ref = bf16[8,45,128]{2,1,0:T(8,128)(2,1)} copy(bf16[8,45,128]{2,0,1:T(8,128)(2,1)} %param.13) | data formatting | bytes 184320 | tf_op args[0]
  3.8 0.7 fusion.1
  4.6 0.9 copy.22
  5.5 1.0 begin.1
  6.6 0.6 copy-done.3
  7.2 87.6 %while.43 = (s32[]{:T(128)}, bf16[384,128]{1,0:T(8,128)(2,1)S(1)}, f32[384,128]{1,0:T(8,128)S(1)}, bf16[2,384,128]{2,1,0:T(8,128)(2,1)S(1)}, bf16[2,384,128]{2,1...) while((s32[]{:T(128)}, bf16[384,128]{1,0:T(8,128)(2,1)S(1)}, ...), condition=%wide.region_5.0_spmd, body=%wide.region_0.0_spmd.sunk | while | flops 3 | bytes 1573265 | solution.py:346
  7.2 0.6 dynamic_slice.8
  8.4 12.7 %conditional.2 = (bf16[384,128]{1,0:T(8,128)(2,1)}, bf16[384,128]{1,0:T(8,128)(2,1)}, bf16[384,128]{1,0:T(8,128)(2,1)}, bf16[384,128]{1,0:T(8,128)(2,1)}) conditional(s32[]{:T(128)} %bitcast.16, bf16[384,128]{1,0:T(8,128)(2,1)S(1)} %get-tuple-element.523.field_in, ...), branch_computations={%region_1.0_spmd, %region_2.0_spmd, %region_3.0_spmd, %region_4.0_... | conditional | bytes 1573056 | solution.py:49
  8.5 2.5 %collective-permute-start.10 = (bf16[384,128]{1,0:T(8,128)(2,1)S(1)}, bf16[384,128]{1,0:T(8,128)(2,1)}, u32[]{:S(2)}, u32[]{:S(2)}) collective-permute-start(bf16[384,128]{1,0:T(8,128)(2,1)S(1)} %param.3), channel_id=1, source_target_pairs={{224,0},{232,8},{240,16},{248,24},{0,32},{8,40},{16,48},{24,56},{3... | collective-permute-start | bytes 294920 | tf_op jit(solution)/shard_map/while/body/eval_jaxpr/cond/branch_3_fun/ppermute | solution.py:23
  11.0 2.5 %collective-permute-start.11 = (bf16[384,128]{1,0:T(8,128)(2,1)S(1)}, bf16[384,128]{1,0:T(8,128)(2,1)}, u32[]{:S(2)}, u32[]{:S(2)}) collective-permute-start(bf16[384,128]{1,0:T(8,128)(2,1)S(1)} %param.3), channel_id=1, source_target_pairs={{232,0},{240,8},{248,16},{0,24},{8,32},{16,40},{24,48},{32,56},{40... | collective-permute-start | bytes 294920 | tf_op jit(solution)/shard_map/while/body/eval_jaxpr/cond/branch_3_fun/ppermute | solution.py:23
  13.5 3.1 %collective-permute-start.12 = (bf16[384,128]{1,0:T(8,128)(2,1)S(1)}, bf16[384,128]{1,0:T(8,128)(2,1)}, u32[]{:S(2)}, u32[]{:S(2)}) collective-permute-start(bf16[384,128]{1,0:T(8,128)(2,1)S(1)} %param.3), channel_id=1, source_target_pairs={{24,0},{32,8},{40,16},{48,24},{56,32},{64,40},{72,48},{80,56},{88,... | collective-permute-start | bytes 294920 | tf_op jit(solution)/shard_map/while/body/eval_jaxpr/cond/branch_3_fun/ppermute | solution.py:23
  16.6 1.6 %collective-permute-start.13 = (bf16[384,128]{1,0:T(8,128)(2,1)S(1)}, bf16[384,128]{1,0:T(8,128)(2,1)}, u32[]{:S(2)}, u32[]{:S(2)}) collective-permute-start(bf16[384,128]{1,0:T(8,128)(2,1)S(1)} %param.3), channel_id=1, source_target_pairs={{32,0},{40,8},{48,16},{56,24},{64,32},{72,40},{80,48},{88,56},{96,... | collective-permute-start | bytes 294920 | tf_op jit(solution)/shard_map/while/body/eval_jaxpr/cond/branch_3_fun/ppermute | solution.py:23
  18.2 3.0 %collective-permute-done.11 = bf16[384,128]{1,0:T(8,128)(2,1)} collective-permute-done((bf16[384,128]{1,0:T(8,128)(2,1)S(1)}, bf16[384,128]{1,0:T(8,128)(2,1)}, u32[]{:S(2)}, u32[]{:S(2)}) %collective-permute-start.11) | collective-permute-done | bytes 98336 | tf_op jit(solution)/shard_map/while/body/eval_jaxpr/cond/branch_3_fun/ppermute | solution.py:23
  21.1 4.1 %stage.5 = (bf16[384,128]{1,0:T(8,128)(2,1)S(1)}, f32[384,128]{1,0:T(8,128)S(1)}, bf16[2,384,128]{2,1,0:T(8,128)(2,1)S(1)}, bf16[2,384,128]{2,1,0:T(8,128)(2,1)S...) custom-call(s32[1]{0:T(128)} %bitcast.15.stage_ref, ...), custom_call_target="tpu_custom_call", output_to_operand_aliasing={{0}: (10, {}), {1}: (11, {}), {2}: (12, {}), {3}: (13, {}),... | custom-call | tf_op jit(solution)/shard_map/while/body/eval_jaxpr/stage/pallas_call | solution.py:334
  25.3 0.6 dynamic_slice.8
  26.5 12.3 %conditional.2 = (bf16[384,128]{1,0:T(8,128)(2,1)}, bf16[384,128]{1,0:T(8,128)(2,1)}, bf16[384,128]{1,0:T(8,128)(2,1)}, bf16[384,128]{1,0:T(8,128)(2,1)}) conditional(s32[]{:T(128)} %bitcast.16, bf16[384,128]{1,0:T(8,128)(2,1)S(1)} %get-tuple-element.523.field_in, ...), branch_computations={%region_1.0_spmd, %region_2.0_spmd, %region_3.0_spmd, %region_4.0_... | conditional | bytes 1573056 | solution.py:49
  26.5 1.4 collective-permute-start.10
  27.9 3.5 %collective-permute-start.11 = (bf16[384,128]{1,0:T(8,128)(2,1)S(1)}, bf16[384,128]{1,0:T(8,128)(2,1)}, u32[]{:S(2)}, u32[]{:S(2)}) collective-permute-start(bf16[384,128]{1,0:T(8,128)(2,1)S(1)} %param.3), channel_id=1, source_target_pairs={{232,0},{240,8},{248,16},{0,24},{8,32},{16,40},{24,48},{32,56},{40... | collective-permute-start | bytes 294920 | tf_op jit(solution)/shard_map/while/body/eval_jaxpr/cond/branch_3_fun/ppermute | solution.py:23
  32.2 2.8 %collective-permute-done.11 = bf16[384,128]{1,0:T(8,128)(2,1)} collective-permute-done((bf16[384,128]{1,0:T(8,128)(2,1)S(1)}, bf16[384,128]{1,0:T(8,128)(2,1)}, u32[]{:S(2)}, u32[]{:S(2)}) %collective-permute-start.11) | collective-permute-done | bytes 98336 | tf_op jit(solution)/shard_map/while/body/eval_jaxpr/cond/branch_3_fun/ppermute | solution.py:23
  35.0 1.6 %collective-permute-done.12 = bf16[384,128]{1,0:T(8,128)(2,1)} collective-permute-done((bf16[384,128]{1,0:T(8,128)(2,1)S(1)}, bf16[384,128]{1,0:T(8,128)(2,1)}, u32[]{:S(2)}, u32[]{:S(2)}) %collective-permute-start.12) | collective-permute-done | bytes 98336 | tf_op jit(solution)/shard_map/while/body/eval_jaxpr/cond/branch_3_fun/ppermute | solution.py:23
  36.5 2.2 %collective-permute-done.13 = bf16[384,128]{1,0:T(8,128)(2,1)} collective-permute-done((bf16[384,128]{1,0:T(8,128)(2,1)S(1)}, bf16[384,128]{1,0:T(8,128)(2,1)}, u32[]{:S(2)}, u32[]{:S(2)}) %collective-permute-start.13) | collective-permute-done | bytes 98336 | tf_op jit(solution)/shard_map/while/body/eval_jaxpr/cond/branch_3_fun/ppermute | solution.py:23
  38.8 4.1 %stage.5 = (bf16[384,128]{1,0:T(8,128)(2,1)S(1)}, f32[384,128]{1,0:T(8,128)S(1)}, bf16[2,384,128]{2,1,0:T(8,128)(2,1)S(1)}, bf16[2,384,128]{2,1,0:T(8,128)(2,1)S...) custom-call(s32[1]{0:T(128)} %bitcast.15.stage_ref, ...), custom_call_target="tpu_custom_call", output_to_operand_aliasing={{0}: (10, {}), {1}: (11, {}), {2}: (12, {}), {3}: (13, {}),... | custom-call | tf_op jit(solution)/shard_map/while/body/eval_jaxpr/stage/pallas_call | solution.py:334
  42.9 0.6 dynamic_slice.8
  44.1 4.3 %conditional.2 = (bf16[384,128]{1,0:T(8,128)(2,1)}, bf16[384,128]{1,0:T(8,128)(2,1)}, bf16[384,128]{1,0:T(8,128)(2,1)}, bf16[384,128]{1,0:T(8,128)(2,1)}) conditional(s32[]{:T(128)} %bitcast.16, bf16[384,128]{1,0:T(8,128)(2,1)S(1)} %get-tuple-element.523.field_in, ...), branch_computations={%region_1.0_spmd, %region_2.0_spmd, %region_3.0_spmd, %region_4.0_... | conditional | bytes 1573056 | solution.py:49
  44.2 0.6 collective-permute-start.1
  44.8 0.6 copy.30
  45.4 0.6 copy.31
  46.1 2.4 %collective-permute-done.1 = bf16[384,128]{1,0:T(8,128)(2,1)} collective-permute-done((bf16[384,128]{1,0:T(8,128)(2,1)S(1)}, bf16[384,128]{1,0:T(8,128)(2,1)}, u32[]{:S(2)}, u32[]{:S(2)}) %collective-permute-start.1) | collective-permute-done | bytes 98336 | tf_op jit(solution)/shard_map/while/body/eval_jaxpr/cond/branch_0_fun/ppermute | solution.py:23
  48.5 4.8 %stage.5 = (bf16[384,128]{1,0:T(8,128)(2,1)S(1)}, f32[384,128]{1,0:T(8,128)S(1)}, bf16[2,384,128]{2,1,0:T(8,128)(2,1)S(1)}, bf16[2,384,128]{2,1,0:T(8,128)(2,1)S...) custom-call(s32[1]{0:T(128)} %bitcast.15.stage_ref, ...), custom_call_target="tpu_custom_call", output_to_operand_aliasing={{0}: (10, {}), {1}: (11, {}), {2}: (12, {}), {3}: (13, {}),... | custom-call | tf_op jit(solution)/shard_map/while/body/eval_jaxpr/stage/pallas_call | solution.py:334
  53.2 0.6 dynamic_slice.8
  54.5 7.1 %conditional.2 = (bf16[384,128]{1,0:T(8,128)(2,1)}, bf16[384,128]{1,0:T(8,128)(2,1)}, bf16[384,128]{1,0:T(8,128)(2,1)}, bf16[384,128]{1,0:T(8,128)(2,1)}) conditional(s32[]{:T(128)} %bitcast.16, bf16[384,128]{1,0:T(8,128)(2,1)S(1)} %get-tuple-element.523.field_in, ...), branch_computations={%region_1.0_spmd, %region_2.0_spmd, %region_3.0_spmd, %region_4.0_... | conditional | bytes 1573056 | solution.py:49
  54.5 0.5 collective-permute-start
  55.1 2.1 %collective-permute-start.1 = (bf16[384,128]{1,0:T(8,128)(2,1)S(1)}, bf16[384,128]{1,0:T(8,128)(2,1)}, u32[]{:S(2)}, u32[]{:S(2)}) collective-permute-start(bf16[384,128]{1,0:T(8,128)(2,1)S(1)} %param), channel_id=1, source_target_pairs={{8,0},{16,8},{24,16},{32,24},{40,32},{48,40},{56,48},{64,56},{72,6... | collective-permute-start | bytes 294920 | tf_op jit(solution)/shard_map/while/body/eval_jaxpr/cond/branch_0_fun/ppermute | solution.py:23
  57.2 0.6 copy.30
  57.8 0.6 copy.31
  58.5 3.1 %collective-permute-done.1 = bf16[384,128]{1,0:T(8,128)(2,1)} collective-permute-done((bf16[384,128]{1,0:T(8,128)(2,1)S(1)}, bf16[384,128]{1,0:T(8,128)(2,1)}, u32[]{:S(2)}, u32[]{:S(2)}) %collective-permute-start.1) | collective-permute-done | bytes 98336 | tf_op jit(solution)/shard_map/while/body/eval_jaxpr/cond/branch_0_fun/ppermute | solution.py:23
  61.6 4.0 %stage.5 = (bf16[384,128]{1,0:T(8,128)(2,1)S(1)}, f32[384,128]{1,0:T(8,128)S(1)}, bf16[2,384,128]{2,1,0:T(8,128)(2,1)S(1)}, bf16[2,384,128]{2,1,0:T(8,128)(2,1)S...) custom-call(s32[1]{0:T(128)} %bitcast.15.stage_ref, ...), custom_call_target="tpu_custom_call", output_to_operand_aliasing={{0}: (10, {}), {1}: (11, {}), {2}: (12, {}), {3}: (13, {}),... | custom-call | tf_op jit(solution)/shard_map/while/body/eval_jaxpr/stage/pallas_call | solution.py:334
  65.6 0.6 dynamic_slice.8
  66.8 9.7 %conditional.2 = (bf16[384,128]{1,0:T(8,128)(2,1)}, bf16[384,128]{1,0:T(8,128)(2,1)}, bf16[384,128]{1,0:T(8,128)(2,1)}, bf16[384,128]{1,0:T(8,128)(2,1)}) conditional(s32[]{:T(128)} %bitcast.16, bf16[384,128]{1,0:T(8,128)(2,1)S(1)} %get-tuple-element.523.field_in, ...), branch_computations={%region_1.0_spmd, %region_2.0_spmd, %region_3.0_spmd, %region_4.0_... | conditional | bytes 1573056 | solution.py:49
  66.9 1.2 collective-permute-start.10
  68.3 3.5 %collective-permute-start.12 = (bf16[384,128]{1,0:T(8,128)(2,1)S(1)}, bf16[384,128]{1,0:T(8,128)(2,1)}, u32[]{:S(2)}, u32[]{:S(2)}) collective-permute-start(bf16[384,128]{1,0:T(8,128)(2,1)S(1)} %param.3), channel_id=1, source_target_pairs={{24,0},{32,8},{40,16},{48,24},{56,32},{64,40},{72,48},{80,56},{88,... | collective-permute-start | bytes 294920 | tf_op jit(solution)/shard_map/while/body/eval_jaxpr/cond/branch_3_fun/ppermute | solution.py:23
  72.3 3.0 %collective-permute-done.11 = bf16[384,128]{1,0:T(8,128)(2,1)} collective-permute-done((bf16[384,128]{1,0:T(8,128)(2,1)S(1)}, bf16[384,128]{1,0:T(8,128)(2,1)}, u32[]{:S(2)}, u32[]{:S(2)}) %collective-permute-start.11) | collective-permute-done | bytes 98336 | tf_op jit(solution)/shard_map/while/body/eval_jaxpr/cond/branch_3_fun/ppermute | solution.py:23
  75.3 1.3 collective-permute-done.13
  76.5 4.0 %stage.5 = (bf16[384,128]{1,0:T(8,128)(2,1)S(1)}, f32[384,128]{1,0:T(8,128)S(1)}, bf16[2,384,128]{2,1,0:T(8,128)(2,1)S(1)}, bf16[2,384,128]{2,1,0:T(8,128)(2,1)S...) custom-call(s32[1]{0:T(128)} %bitcast.15.stage_ref, ...), custom_call_target="tpu_custom_call", output_to_operand_aliasing={{0}: (10, {}), {1}: (11, {}), {2}: (12, {}), {3}: (13, {}),... | custom-call | tf_op jit(solution)/shard_map/while/body/eval_jaxpr/stage/pallas_call | solution.py:334
  80.5 0.6 dynamic_slice.8
  81.8 9.6 %conditional.2 = (bf16[384,128]{1,0:T(8,128)(2,1)}, bf16[384,128]{1,0:T(8,128)(2,1)}, bf16[384,128]{1,0:T(8,128)(2,1)}, bf16[384,128]{1,0:T(8,128)(2,1)}) conditional(s32[]{:T(128)} %bitcast.16, bf16[384,128]{1,0:T(8,128)(2,1)S(1)} %get-tuple-element.523.field_in, ...), branch_computations={%region_1.0_spmd, %region_2.0_spmd, %region_3.0_spmd, %region_4.0_... | conditional | bytes 1573056 | solution.py:49
  81.8 1.4 collective-permute-start.10
  83.2 1.1 collective-permute-start.11
  84.3 2.8 %collective-permute-start.12 = (bf16[384,128]{1,0:T(8,128)(2,1)S(1)}, bf16[384,128]{1,0:T(8,128)(2,1)}, u32[]{:S(2)}, u32[]{:S(2)}) collective-permute-start(bf16[384,128]{1,0:T(8,128)(2,1)S(1)} %param.3), channel_id=1, source_target_pairs={{24,0},{32,8},{40,16},{48,24},{56,32},{64,40},{72,48},{80,56},{88,... | collective-permute-start | bytes 294920 | tf_op jit(solution)/shard_map/while/body/eval_jaxpr/cond/branch_3_fun/ppermute | solution.py:23
  87.1 1.1 collective-permute-start.13
  88.2 2.2 %collective-permute-done.11 = bf16[384,128]{1,0:T(8,128)(2,1)} collective-permute-done((bf16[384,128]{1,0:T(8,128)(2,1)S(1)}, bf16[384,128]{1,0:T(8,128)(2,1)}, u32[]{:S(2)}, u32[]{:S(2)}) %collective-permute-start.11) | collective-permute-done | bytes 98336 | tf_op jit(solution)/shard_map/while/body/eval_jaxpr/cond/branch_3_fun/ppermute | solution.py:23
  90.4 1.0 collective-permute-done.13
  91.4 3.2 %stage.5 = (bf16[384,128]{1,0:T(8,128)(2,1)S(1)}, f32[384,128]{1,0:T(8,128)S(1)}, bf16[2,384,128]{2,1,0:T(8,128)(2,1)S(1)}, bf16[2,384,128]{2,1,0:T(8,128)(2,1)S...) custom-call(s32[1]{0:T(128)} %bitcast.15.stage_ref, ...), custom_call_target="tpu_custom_call", output_to_operand_aliasing={{0}: (10, {}), {1}: (11, {}), {2}: (12, {}), {3}: (13, {}),... | custom-call | tf_op jit(solution)/shard_map/while/body/eval_jaxpr/stage/pallas_call | solution.py:334
  94.8 23.5 %all_to_all.5 = bf16[32,112,128]{2,1,0:T(8,128)(2,1)S(1)} all-to-all(bf16[32,112,128]{2,1,0:T(8,128)(2,1)S(1)} %bitcast.18), channel_id=1, replica_groups=mesh['z'=8,'xl'=2,'core'=2,'mem'=8] {'mem','xl','core'}, dimensions={0} | all-to-all | bytes 1835008 | tf_op jit(solution)/shard_map/all_to_all | solution.py:253
  118.5 2.8 %collective-permute-start.15 = (bf16[112,128]{1,0:T(8,128)(2,1)S(1)}, bf16[112,128]{1,0:T(8,128)(2,1)S(1)}, u32[]{:S(2)}, u32[]{:S(2)}) collective-permute-start(bf16[112,128]{1,0:T(8,128)(2,1)S(1)} %reduce_sum.12), channel_id=1, source_target_pairs={{64,0},{96,32},{0,64},{32,96},{192,128},{224,160},{128,192},{160,2... | collective-permute-start | bytes 86024 | tf_op jit(solution)/shard_map/ppermute | solution.py:258
  121.3 0.8 collective-permute-start.16
  122.1 3.8 %collective-permute-start.17 = (bf16[112,128]{1,0:T(8,128)(2,1)S(1)}, bf16[112,128]{1,0:T(8,128)(2,1)S(1)}, u32[]{:S(2)}, u32[]{:S(2)}) collective-permute-start(bf16[112,128]{1,0:T(8,128)(2,1)S(1)} %reduce_sum.12), channel_id=1, source_target_pairs={{128,0},{160,32},{192,64},{224,96},{0,128},{32,160},{64,192},{96,2... | collective-permute-start | bytes 86024 | tf_op jit(solution)/shard_map/ppermute | solution.py:258
  125.9 4.9 %collective-permute-start.19 = (bf16[112,128]{1,0:T(8,128)(2,1)S(1)}, bf16[112,128]{1,0:T(8,128)(2,1)S(1)}, u32[]{:S(2)}, u32[]{:S(2)}) collective-permute-start(bf16[112,128]{1,0:T(8,128)(2,1)S(1)} %reduce_sum.12), channel_id=1, source_target_pairs={{192,0},{224,32},{128,64},{160,96},{64,128},{96,160},{0,192},{32,2... | collective-permute-start | bytes 86024 | tf_op jit(solution)/shard_map/ppermute | solution.py:258
  130.8 0.7 copy_bitcast_fusion.1
  131.5 0.7 collective-permute-done.18
  132.2 2.6 %collective-permute-done.20 = bf16[112,128]{1,0:T(8,128)(2,1)S(1)} collective-permute-done((bf16[112,128]{1,0:T(8,128)(2,1)S(1)}, bf16[112,128]{1,0:T(8,128)(2,1)S(1)}, u32[]{:S(2)}, u32[]{:S(2)}) %collective-permute-start.20) | collective-permute-done | bytes 28704 | tf_op jit(solution)/shard_map/ppermute | solution.py:258
  134.8 8.3 %all-gather = bf16[448,128]{1,0:T(8,128)(2,1)S(1)} all-gather(bf16[112,128]{1,0:T(8,128)(2,1)S(1)} %add_convert_fusion), channel_id=2, replica_groups=mesh['z'=8,'xl'=2,'core'=2,'mem'=8] {'xl','core'}, dimensions={0}, use_global_device_ids=true | all-gather | bytes 143360 | tf_op jit(solution)/shard_map/all_gather | solution.py:261
  143.2 0.7 convert_multiply_fusion
  (34 shorter events, 2.2 us)
Async XLA Ops:
  0.6 5.9 %copy-start = (bf16[3,128,512]{2,1,0:T(8,128)(2,1)S(1)}, bf16[3,128,512]{2,1,0:T(8,128)(2,1)}, u32[]{:S(2)}) copy-start(bf16[3,128,512]{2,1,0:T(8,128)(2,1)} %param.17) | copy-start | bytes 1179652
  0.6 5.9 %copy-start.1 = (bf16[3,512,128]{2,1,0:T(8,128)(2,1)S(1)}, bf16[3,512,128]{2,1,0:T(8,128)(2,1)}, u32[]{:S(2)}) copy-start(bf16[3,512,128]{2,1,0:T(8,128)(2,1)} %param.18) | copy-start | bytes 1179652
  6.5 0.7 copy-start.3
  8.5 9.7 %collective-permute-start.10 = (bf16[384,128]{1,0:T(8,128)(2,1)S(1)}, bf16[384,128]{1,0:T(8,128)(2,1)}, u32[]{:S(2)}, u32[]{:S(2)}) collective-permute-start(bf16[384,128]{1,0:T(8,128)(2,1)S(1)} %param.3), channel_id=1, source_target_pairs={{224,0},{232,8},{240,16},{248,24},{0,32},{8,40},{16,48},{24,56},{3... | collective-permute-start | bytes 294920 | tf_op jit(solution)/shard_map/while/body/eval_jaxpr/cond/branch_3_fun/ppermute | solution.py:23
  11.0 10.1 %collective-permute-start.11 = (bf16[384,128]{1,0:T(8,128)(2,1)S(1)}, bf16[384,128]{1,0:T(8,128)(2,1)}, u32[]{:S(2)}, u32[]{:S(2)}) collective-permute-start(bf16[384,128]{1,0:T(8,128)(2,1)S(1)} %param.3), channel_id=1, source_target_pairs={{232,0},{240,8},{248,16},{0,24},{8,32},{16,40},{24,48},{32,56},{40... | collective-permute-start | bytes 294920 | tf_op jit(solution)/shard_map/while/body/eval_jaxpr/cond/branch_3_fun/ppermute | solution.py:23
  13.5 7.7 %collective-permute-start.12 = (bf16[384,128]{1,0:T(8,128)(2,1)S(1)}, bf16[384,128]{1,0:T(8,128)(2,1)}, u32[]{:S(2)}, u32[]{:S(2)}) collective-permute-start(bf16[384,128]{1,0:T(8,128)(2,1)S(1)} %param.3), channel_id=1, source_target_pairs={{24,0},{32,8},{40,16},{48,24},{56,32},{64,40},{72,48},{80,56},{88,... | collective-permute-start | bytes 294920 | tf_op jit(solution)/shard_map/while/body/eval_jaxpr/cond/branch_3_fun/ppermute | solution.py:23
  16.6 4.5 %collective-permute-start.13 = (bf16[384,128]{1,0:T(8,128)(2,1)S(1)}, bf16[384,128]{1,0:T(8,128)(2,1)}, u32[]{:S(2)}, u32[]{:S(2)}) collective-permute-start(bf16[384,128]{1,0:T(8,128)(2,1)S(1)} %param.3), channel_id=1, source_target_pairs={{32,0},{40,8},{48,16},{56,24},{64,32},{72,40},{80,48},{88,56},{96,... | collective-permute-start | bytes 294920 | tf_op jit(solution)/shard_map/while/body/eval_jaxpr/cond/branch_3_fun/ppermute | solution.py:23
  26.5 5.7 %collective-permute-start.10 = (bf16[384,128]{1,0:T(8,128)(2,1)S(1)}, bf16[384,128]{1,0:T(8,128)(2,1)}, u32[]{:S(2)}, u32[]{:S(2)}) collective-permute-start(bf16[384,128]{1,0:T(8,128)(2,1)S(1)} %param.3), channel_id=1, source_target_pairs={{224,0},{232,8},{240,16},{248,24},{0,32},{8,40},{16,48},{24,56},{3... | collective-permute-start | bytes 294920 | tf_op jit(solution)/shard_map/while/body/eval_jaxpr/cond/branch_3_fun/ppermute | solution.py:23
  27.9 7.1 %collective-permute-start.11 = (bf16[384,128]{1,0:T(8,128)(2,1)S(1)}, bf16[384,128]{1,0:T(8,128)(2,1)}, u32[]{:S(2)}, u32[]{:S(2)}) collective-permute-start(bf16[384,128]{1,0:T(8,128)(2,1)S(1)} %param.3), channel_id=1, source_target_pairs={{232,0},{240,8},{248,16},{0,24},{8,32},{16,40},{24,48},{32,56},{40... | collective-permute-start | bytes 294920 | tf_op jit(solution)/shard_map/while/body/eval_jaxpr/cond/branch_3_fun/ppermute | solution.py:23
  31.4 5.2 %collective-permute-start.12 = (bf16[384,128]{1,0:T(8,128)(2,1)S(1)}, bf16[384,128]{1,0:T(8,128)(2,1)}, u32[]{:S(2)}, u32[]{:S(2)}) collective-permute-start(bf16[384,128]{1,0:T(8,128)(2,1)S(1)} %param.3), channel_id=1, source_target_pairs={{24,0},{32,8},{40,16},{48,24},{56,32},{64,40},{72,48},{80,56},{88,... | collective-permute-start | bytes 294920 | tf_op jit(solution)/shard_map/while/body/eval_jaxpr/cond/branch_3_fun/ppermute | solution.py:23
  31.7 7.0 %collective-permute-start.13 = (bf16[384,128]{1,0:T(8,128)(2,1)S(1)}, bf16[384,128]{1,0:T(8,128)(2,1)}, u32[]{:S(2)}, u32[]{:S(2)}) collective-permute-start(bf16[384,128]{1,0:T(8,128)(2,1)S(1)} %param.3), channel_id=1, source_target_pairs={{32,0},{40,8},{48,16},{56,24},{64,32},{72,40},{80,48},{88,56},{96,... | collective-permute-start | bytes 294920 | tf_op jit(solution)/shard_map/while/body/eval_jaxpr/cond/branch_3_fun/ppermute | solution.py:23
  44.2 1.9 %collective-permute-start = (bf16[384,128]{1,0:T(8,128)(2,1)S(1)}, bf16[384,128]{1,0:T(8,128)(2,1)}, u32[]{:S(2)}, u32[]{:S(2)}) collective-permute-start(bf16[384,128]{1,0:T(8,128)(2,1)S(1)} %param), channel_id=1, source_target_pairs={{248,0},{0,8},{8,16},{16,24},{24,32},{32,40},{40,48},{48,56},{56,6... | collective-permute-start | bytes 294920 | tf_op jit(solution)/shard_map/while/body/eval_jaxpr/cond/branch_0_fun/ppermute | solution.py:23
  44.2 4.2 %collective-permute-start.1 = (bf16[384,128]{1,0:T(8,128)(2,1)S(1)}, bf16[384,128]{1,0:T(8,128)(2,1)}, u32[]{:S(2)}, u32[]{:S(2)}) collective-permute-start(bf16[384,128]{1,0:T(8,128)(2,1)S(1)} %param), channel_id=1, source_target_pairs={{8,0},{16,8},{24,16},{32,24},{40,32},{48,40},{56,48},{64,56},{72,6... | collective-permute-start | bytes 294920 | tf_op jit(solution)/shard_map/while/body/eval_jaxpr/cond/branch_0_fun/ppermute | solution.py:23
  54.5 4.0 %collective-permute-start = (bf16[384,128]{1,0:T(8,128)(2,1)S(1)}, bf16[384,128]{1,0:T(8,128)(2,1)}, u32[]{:S(2)}, u32[]{:S(2)}) collective-permute-start(bf16[384,128]{1,0:T(8,128)(2,1)S(1)} %param), channel_id=1, source_target_pairs={{248,0},{0,8},{8,16},{16,24},{24,32},{32,40},{40,48},{48,56},{56,6... | collective-permute-start | bytes 294920 | tf_op jit(solution)/shard_map/while/body/eval_jaxpr/cond/branch_0_fun/ppermute | solution.py:23
  55.1 6.5 %collective-permute-start.1 = (bf16[384,128]{1,0:T(8,128)(2,1)S(1)}, bf16[384,128]{1,0:T(8,128)(2,1)}, u32[]{:S(2)}, u32[]{:S(2)}) collective-permute-start(bf16[384,128]{1,0:T(8,128)(2,1)S(1)} %param), channel_id=1, source_target_pairs={{8,0},{16,8},{24,16},{32,24},{40,32},{48,40},{56,48},{64,56},{72,6... | collective-permute-start | bytes 294920 | tf_op jit(solution)/shard_map/while/body/eval_jaxpr/cond/branch_0_fun/ppermute | solution.py:23
  66.9 5.4 %collective-permute-start.10 = (bf16[384,128]{1,0:T(8,128)(2,1)S(1)}, bf16[384,128]{1,0:T(8,128)(2,1)}, u32[]{:S(2)}, u32[]{:S(2)}) collective-permute-start(bf16[384,128]{1,0:T(8,128)(2,1)S(1)} %param.3), channel_id=1, source_target_pairs={{224,0},{232,8},{240,16},{248,24},{0,32},{8,40},{16,48},{24,56},{3... | collective-permute-start | bytes 294920 | tf_op jit(solution)/shard_map/while/body/eval_jaxpr/cond/branch_3_fun/ppermute | solution.py:23
  68.0 7.2 %collective-permute-start.11 = (bf16[384,128]{1,0:T(8,128)(2,1)S(1)}, bf16[384,128]{1,0:T(8,128)(2,1)}, u32[]{:S(2)}, u32[]{:S(2)}) collective-permute-start(bf16[384,128]{1,0:T(8,128)(2,1)S(1)} %param.3), channel_id=1, source_target_pairs={{232,0},{240,8},{248,16},{0,24},{8,32},{16,40},{24,48},{32,56},{40... | collective-permute-start | bytes 294920 | tf_op jit(solution)/shard_map/while/body/eval_jaxpr/cond/branch_3_fun/ppermute | solution.py:23
  68.3 6.9 %collective-permute-start.12 = (bf16[384,128]{1,0:T(8,128)(2,1)S(1)}, bf16[384,128]{1,0:T(8,128)(2,1)}, u32[]{:S(2)}, u32[]{:S(2)}) collective-permute-start(bf16[384,128]{1,0:T(8,128)(2,1)S(1)} %param.3), channel_id=1, source_target_pairs={{24,0},{32,8},{40,16},{48,24},{56,32},{64,40},{72,48},{80,56},{88,... | collective-permute-start | bytes 294920 | tf_op jit(solution)/shard_map/while/body/eval_jaxpr/cond/branch_3_fun/ppermute | solution.py:23
  71.9 4.6 %collective-permute-start.13 = (bf16[384,128]{1,0:T(8,128)(2,1)S(1)}, bf16[384,128]{1,0:T(8,128)(2,1)}, u32[]{:S(2)}, u32[]{:S(2)}) collective-permute-start(bf16[384,128]{1,0:T(8,128)(2,1)S(1)} %param.3), channel_id=1, source_target_pairs={{32,0},{40,8},{48,16},{56,24},{64,32},{72,40},{80,48},{88,56},{96,... | collective-permute-start | bytes 294920 | tf_op jit(solution)/shard_map/while/body/eval_jaxpr/cond/branch_3_fun/ppermute | solution.py:23
  81.8 6.4 %collective-permute-start.10 = (bf16[384,128]{1,0:T(8,128)(2,1)S(1)}, bf16[384,128]{1,0:T(8,128)(2,1)}, u32[]{:S(2)}, u32[]{:S(2)}) collective-permute-start(bf16[384,128]{1,0:T(8,128)(2,1)S(1)} %param.3), channel_id=1, source_target_pairs={{224,0},{232,8},{240,16},{248,24},{0,32},{8,40},{16,48},{24,56},{3... | collective-permute-start | bytes 294920 | tf_op jit(solution)/shard_map/while/body/eval_jaxpr/cond/branch_3_fun/ppermute | solution.py:23
  83.2 7.2 %collective-permute-start.11 = (bf16[384,128]{1,0:T(8,128)(2,1)S(1)}, bf16[384,128]{1,0:T(8,128)(2,1)}, u32[]{:S(2)}, u32[]{:S(2)}) collective-permute-start(bf16[384,128]{1,0:T(8,128)(2,1)S(1)} %param.3), channel_id=1, source_target_pairs={{232,0},{240,8},{248,16},{0,24},{8,32},{16,40},{24,48},{32,56},{40... | collective-permute-start | bytes 294920 | tf_op jit(solution)/shard_map/while/body/eval_jaxpr/cond/branch_3_fun/ppermute | solution.py:23
  84.3 6.1 %collective-permute-start.12 = (bf16[384,128]{1,0:T(8,128)(2,1)S(1)}, bf16[384,128]{1,0:T(8,128)(2,1)}, u32[]{:S(2)}, u32[]{:S(2)}) collective-permute-start(bf16[384,128]{1,0:T(8,128)(2,1)S(1)} %param.3), channel_id=1, source_target_pairs={{24,0},{32,8},{40,16},{48,24},{56,32},{64,40},{72,48},{80,56},{88,... | collective-permute-start | bytes 294920 | tf_op jit(solution)/shard_map/while/body/eval_jaxpr/cond/branch_3_fun/ppermute | solution.py:23
  87.1 4.3 %collective-permute-start.13 = (bf16[384,128]{1,0:T(8,128)(2,1)S(1)}, bf16[384,128]{1,0:T(8,128)(2,1)}, u32[]{:S(2)}, u32[]{:S(2)}) collective-permute-start(bf16[384,128]{1,0:T(8,128)(2,1)S(1)} %param.3), channel_id=1, source_target_pairs={{32,0},{40,8},{48,16},{56,24},{64,32},{72,40},{80,48},{88,56},{96,... | collective-permute-start | bytes 294920 | tf_op jit(solution)/shard_map/while/body/eval_jaxpr/cond/branch_3_fun/ppermute | solution.py:23
  118.3 12.5 %copy-start.2 = (bf16[8,45,128]{2,1,0:T(8,128)(2,1)S(1)}, bf16[8,45,128]{2,1,0:T(8,128)(2,1)}, u32[]{:S(2)}) copy-start(bf16[8,45,128]{2,1,0:T(8,128)(2,1)} %get-tuple-element.300) | copy-start | bytes 276484
  118.4 7.5 %collective-permute-start.14 = (bf16[112,128]{1,0:T(8,128)(2,1)S(1)}, bf16[112,128]{1,0:T(8,128)(2,1)S(1)}, u32[]{:S(2)}, u32[]{:S(2)}) collective-permute-start(bf16[112,128]{1,0:T(8,128)(2,1)S(1)} %reduce_sum.12), channel_id=1, source_target_pairs={{32,0},{0,32},{96,64},{64,96},{160,128},{128,160},{224,192},{192,2... | collective-permute-start | bytes 86024 | tf_op jit(solution)/shard_map/ppermute | solution.py:258
  118.5 12.2 %collective-permute-start.15 = (bf16[112,128]{1,0:T(8,128)(2,1)S(1)}, bf16[112,128]{1,0:T(8,128)(2,1)S(1)}, u32[]{:S(2)}, u32[]{:S(2)}) collective-permute-start(bf16[112,128]{1,0:T(8,128)(2,1)S(1)} %reduce_sum.12), channel_id=1, source_target_pairs={{64,0},{96,32},{0,64},{32,96},{192,128},{224,160},{128,192},{160,2... | collective-permute-start | bytes 86024 | tf_op jit(solution)/shard_map/ppermute | solution.py:258
  121.3 10.2 %collective-permute-start.16 = (bf16[112,128]{1,0:T(8,128)(2,1)S(1)}, bf16[112,128]{1,0:T(8,128)(2,1)S(1)}, u32[]{:S(2)}, u32[]{:S(2)}) collective-permute-start(bf16[112,128]{1,0:T(8,128)(2,1)S(1)} %reduce_sum.12), channel_id=1, source_target_pairs={{96,0},{64,32},{32,64},{0,96},{224,128},{192,160},{160,192},{128,2... | collective-permute-start | bytes 86024 | tf_op jit(solution)/shard_map/ppermute | solution.py:258
  122.1 9.4 %collective-permute-start.17 = (bf16[112,128]{1,0:T(8,128)(2,1)S(1)}, bf16[112,128]{1,0:T(8,128)(2,1)S(1)}, u32[]{:S(2)}, u32[]{:S(2)}) collective-permute-start(bf16[112,128]{1,0:T(8,128)(2,1)S(1)} %reduce_sum.12), channel_id=1, source_target_pairs={{128,0},{160,32},{192,64},{224,96},{0,128},{32,160},{64,192},{96,2... | collective-permute-start | bytes 86024 | tf_op jit(solution)/shard_map/ppermute | solution.py:258
  125.9 6.3 %collective-permute-start.18 = (bf16[112,128]{1,0:T(8,128)(2,1)S(1)}, bf16[112,128]{1,0:T(8,128)(2,1)S(1)}, u32[]{:S(2)}, u32[]{:S(2)}) collective-permute-start(bf16[112,128]{1,0:T(8,128)(2,1)S(1)} %reduce_sum.12), channel_id=1, source_target_pairs={{160,0},{128,32},{224,64},{192,96},{32,128},{0,160},{96,192},{64,2... | collective-permute-start | bytes 86024 | tf_op jit(solution)/shard_map/ppermute | solution.py:258
  125.9 6.3 %collective-permute-start.19 = (bf16[112,128]{1,0:T(8,128)(2,1)S(1)}, bf16[112,128]{1,0:T(8,128)(2,1)S(1)}, u32[]{:S(2)}, u32[]{:S(2)}) collective-permute-start(bf16[112,128]{1,0:T(8,128)(2,1)S(1)} %reduce_sum.12), channel_id=1, source_target_pairs={{192,0},{224,32},{128,64},{160,96},{64,128},{96,160},{0,192},{32,2... | collective-permute-start | bytes 86024 | tf_op jit(solution)/shard_map/ppermute | solution.py:258
  130.8 4.1 %collective-permute-start.20 = (bf16[112,128]{1,0:T(8,128)(2,1)S(1)}, bf16[112,128]{1,0:T(8,128)(2,1)S(1)}, u32[]{:S(2)}, u32[]{:S(2)}) collective-permute-start(bf16[112,128]{1,0:T(8,128)(2,1)S(1)} %reduce_sum.12), channel_id=1, source_target_pairs={{224,0},{192,32},{160,64},{128,96},{96,128},{64,160},{32,192},{0,2... | collective-permute-start | bytes 86024 | tf_op jit(solution)/shard_map/ppermute | solution.py:258
where the time goes:
time: 145 us; the launch traced here: 144 us
  starting transfers between devices  42.5 us (29%)
  blocking collectives  31.9 us (22%)
  waiting for transfers between devices  26.1 us (18%)
  Pallas kernels  25.1 us (17%)
  local copies, waits for them, and re-layouts  11.6 us (8%)
  loops' own time  4.41 us (3%)
  other arithmetic  1.61 us (1%)
    ppermute x20, starting transfers between devices, passed_along(): return lax.ppermute(block, axis, route)  30.2 us
    pallas_call x6, Pallas kernels, step(): stage_call(stage.reshape(1), spacing_per_tier, *blocks, mixer_entry_proje...  24.1 us
    all_to_all x1, blocking collectives, total_over_all(): lax.all_to_all(terms.reshape(places, each, size.chans), ('mem',) + PLANE,...  23.5 us
    ppermute x20, waiting for transfers between devices, passed_along(): return lax.ppermute(block, axis, route)  22.8 us
    ppermute x7, starting transfers between devices, total_over_all(): lax.ppermute(mine, 'z', [(i ^ flip, i) for i in planes]).astype(F32)  12.3 us
    all_gather x1, blocking collectives, total_over_all(): lax.all_gather(came[0].astype(BF16), PLANE).reshape(size.share, size.chans)  8.35 us
    another operation x1, loops' own time, per_device(): state = lax.fori_loop(0, 2 * LAYERS, step, tuple(state))  4.23 us
    unnamed x10, local copies, waits for them, and re-layouts  3.79 us
  transfers between devices with their start and end apart: 27, of which 14 were waited for; matrix products, arithmetic and copies ran while one was open for 2% of the time, Pallas kernels for 0%

commit v1 on v0

--- a/solution.py
+++ b/solution.py
@@ -111,15 +111,40 @@
     return values * jax.nn.sigmoid(values)
 
 
-def begin_body(size, a_ref, b_ref, field, *unwritten):
-    padded_into(size, field, lambda row: a_ref[row].astype(F32) + b_ref[row].astype(F32))
+def turned_into(size, scratch, out, values):
+    scratch[...] = values.astype(F32).reshape(size.ncols * size.rows, size.chans)
+    for row in range(size.rows):
+        at = row * size.pitch
+        out[pl.ds(at, size.ncols), :] = scratch[pl.ds(row, size.ncols, stride=size.rows), :].astype(
+            out.dtype
+        )
+
+
+def terms_pieces(size, layer):
+    count = 9 * size.chans // size.members
+    pieces = []
+    for member in range(size.members):
+        row = layer * count
+        while row < (layer + 1) * count:
+            half = row // size.each
+            end = min((half + 1) * size.each, (layer + 1) * count)
+            to = (half * size.members + member) * size.each
+            pieces.append((member * count + row - layer * count, to + row % size.each, end - row))
+            row = end
+    return pieces
+
+
+def begin_body(size, a_ref, b_ref, *refs):
+    field, scratch = refs[0], refs[-1]
+    field[...] = jnp.zeros(field.shape, field.dtype)
+    turned_into(size, scratch, field, a_ref[...].astype(F32) + b_ref[...].astype(F32))
 
 
 def stage_body(
     size, stage_ref, spacing_ref, fl, nl, nu, fu, entry, leave, cot, conv, field_in, grad_in, *refs
 ):
     field, grad_out, hidden, mixed, pre_conv, lower, upper, terms, outcome, first = refs[8:18]
-    left, middle, right, back, kernel, own, narrow, pre, before, after, found, block, sems = refs[18:]
+    left, middle, right, back, kernel, own, narrow, pre, before, after, found, block, wide, sems = refs[18:]
     stage = stage_ref[0]
     forward = stage < LAYERS
     turn = stage == LAYERS - 1
@@ -181,7 +206,8 @@
             unpadded_into(size, block, total)
             copy = pltpu.make_async_copy(block, outcome, sems.at[6])
             copy.start()
-            padded_into(size, back, lambda row: cot[row])
+            back[...] = jnp.zeros(back.shape, back.dtype)
+            turned_into(size, wide, back, cot[...])
             copy.wait()
 
     @pl.when(~forward)
@@ -225,21 +251,23 @@
             found[pl.ds(tap * chans, chans), :] = values[:, tap * chans : (tap + 1) * chans].T.astype(
                 BF16
             )
-        count = 9 * chans // size.members
-        copies = []
-        for member in range(size.members):
-            to = pl.multiple_of(member * size.share + at * count, 16)
-            copies.append(
-                pltpu.make_async_copy(
-                    found.at[pl.ds(member * count, count)],
-                    terms.at[pl.ds(to, count)],
-                    sems.at[7 + member],
-                )
-            )
-        for copy in copies:
-            copy.start()
-        for copy in copies:
-            copy.wait()
+        for index in range(LAYERS):
+
+            @pl.when(at == index)
+            def _(index=index):
+                copies = []
+                for begin, to, count in terms_pieces(size, index):
+                    copies.append(
+                        pltpu.make_async_copy(
+                            found.at[pl.ds(begin, count)],
+                            terms.at[pl.ds(to, count)],
+                            sems.at[7 + len(copies)],
+                        )
+                    )
+                for copy in copies:
+                    copy.start()
+                for copy in copies:
+                    copy.wait()
 
 
 VMEM_SPEC = pl.BlockSpec(memory_space=pltpu.VMEM)
@@ -248,17 +276,18 @@
 
 
 def total_over_all(size, terms):
-    places = size.members * 4
-    each = terms.shape[0] // places
-    terms = lax.all_to_all(terms.reshape(places, each, size.chans), ("mem",) + PLANE, 0, 0)
-    mine = jnp.sum(terms.astype(F32), axis=0).astype(BF16)
-    planes = range(lax.axis_size("z"))
-    came = [mine.astype(F32)]
-    for flip in planes[1:]:
-        came.append(lax.ppermute(mine, "z", [(i ^ flip, i) for i in planes]).astype(F32))
-    while len(came) > 1:
-        came = [a + b for a, b in zip(came[::2], came[1::2])]
-    full = lax.all_gather(came[0].astype(BF16), PLANE).reshape(size.share, size.chans)
+    terms = terms.reshape(2, size.members * size.each, size.chans)
+    terms = jnp.sum(lax.all_to_all(terms, "core", 0, 0).astype(F32), axis=0).astype(BF16)
+    terms = terms.reshape(size.members, size.each, size.chans)
+    total = jnp.sum(lax.all_to_all(terms, "mem", 0, 0).astype(F32), axis=0).astype(BF16)
+    depth = lax.axis_size("z")
+    swaps = [("xl", [1, 0])]
+    swaps += [("z", [i ^ 1 for i in range(depth)]), ("z", [i ^ 2 for i in range(depth)])]
+    swaps += [("z", [depth - 1 - i for i in range(depth)])]
+    for axis, partner in swaps:
+        other = lax.ppermute(total, axis, list(enumerate(partner)))
+        total = (total.astype(F32) + other.astype(F32)).astype(BF16)
+    full = lax.all_gather(total, "core").reshape(2 * size.each, size.chans)
     own = 9 * size.chans // size.members
     return full[: LAYERS * own].reshape(LAYERS, own, size.chans).astype(F32)
 
@@ -276,9 +305,13 @@
     size = Sizes(rows, ncols, chans, mixer_entry_projection.shape[2])
     size.hops = (MAXD + ncols - 1) // ncols
     size.members = lax.axis_size("mem")
-    size.share = (LAYERS * 9 * chans // size.members + 63) // 64 * 64
+    size.each = (LAYERS * 9 * chans // size.members + 31) // 32 * 16
+    size.pieces = max(len(terms_pieces(size, layer)) for layer in range(LAYERS))
     tall = (size.cells + 2 * size.pitch, chans)
     cells = (size.cells, chans)
+
+    def columns_first(values):
+        return jnp.swapaxes(values, 0, 1)
 
     def array(*shape, dtype=BF16):
         return jax.ShapeDtypeStruct(shape, dtype)
@@ -291,7 +324,7 @@
         array(LAYERS - 1, *cells, dtype=F32),
         array(LAYERS - 1, *tall),
         array(LAYERS - 1, *tall),
-        array(size.members * size.share, chans),
+        array(2 * size.members * size.each, chans),
         array(rows, ncols, chans),
         array(rows, ncols, chans),
     ]
@@ -301,10 +334,14 @@
         out_shape=kinds,
         in_specs=[VMEM_SPEC] * 2,
         out_specs=[VMEM_SPEC] + [ANY_SPEC] * (held - 1),
+        scratch_shapes=[pltpu.VMEM((rows * ncols, chans), F32)],
         name="begin",
-    )(assimilated_snapshot, stochastic_displacement[0])
-    near = sum((spacing_per_tier > hop * ncols).astype(jnp.int32) for hop in range(1, size.hops))
-    near = jnp.concatenate([near, near[::-1]])
+    )(columns_first(assimilated_snapshot), columns_first(stochastic_displacement[0]))
+    near = [
+        sum((spacing_per_tier[i] > hop * ncols).astype(jnp.int32) for hop in range(1, size.hops))
+        for i in range(LAYERS)
+    ]
+    code = sum(n << (4 * i) for i, n in enumerate(near + near[::-1]))
     state_specs = [VMEM_SPEC] * 2 + [ANY_SPEC] * (held - 2)
     stage_call = pl.pallas_call(
         functools.partial(stage_body, size),
@@ -322,28 +359,31 @@
             pltpu.VMEM(tall, BF16),
             pltpu.VMEM((9 * chans, chans), BF16),
             pltpu.VMEM((rows, ncols, chans), BF16),
-            pltpu.SemaphoreType.DMA((7 + size.members,)),
+            pltpu.VMEM((rows * ncols, chans), F32),
+            pltpu.SemaphoreType.DMA((7 + size.pieces,)),
         ],
         input_output_aliases={10 + i: i for i in range(held)},
         name="stage",
     )
 
     def step(stage, state):
-        blocks = exchange(state[0], near[stage], ncols)
-        return tuple(
-            stage_call(
+        *state, code = state
+        blocks = exchange(state[0], code & 15, ncols)
+        return (
+            *stage_call(
                 stage.reshape(1),
                 spacing_per_tier,
                 *blocks,
                 mixer_entry_projection,
                 mixer_exit_projection,
-                outcome_cotangent_vector[0],
+                columns_first(outcome_cotangent_vector[0]),
                 spatial_window_coefficients,
                 *state,
-            )
+            ),
+            code >> 4,
         )
 
-    state = lax.fori_loop(0, 2 * LAYERS, step, tuple(state))
+    state = lax.fori_loop(0, 2 * LAYERS, step, (*state, code))
     share = total_over_all(size, state[7])
     member_count = size.members * stochastic_displacement.shape[0]
     scale = 1.0 / math.sqrt(member_count * rows * ncols * lax.axis_size(LON))

time: 145 us -> 139 us (0.959)
  starting transfers between devices: 42.5 us -> 34 us
  waiting for transfers between devices: 26.1 us -> 33.6 us
  local copies, waits for them, and re-layouts: 11.6 us -> 5.28 us
  between operations: 0.71 us -> 6.55 us
  loops' own time: 4.41 us -> 0.54 us
    ppermute x7 -> x4, starting transfers between devices: 12.3 us -> 2.53 us  [total_over_all(): other = lax.ppermute(total, axis, list(enumerate(partner)))]
    ppermute x7 -> x4, waiting for transfers between devices: 3.33 us -> 12.3 us  [total_over_all(): other = lax.ppermute(total, axis, list(enumerate(partner)))]
    another operation x1, loops' own time: 4.23 us -> 0.39 us  [per_device(): state = lax.fori_loop(0, 2 * LAYERS, step, (*state, code))]
    dynamic_slice x6 -> x0, local copies, waits for them, and re-layouts: 3.51 us -> none  [step(): blocks = exchange(state[0], near[stage], ncols)]
    unnamed x10 -> x4, local copies, waits for them, and re-layouts: 3.79 us -> 0.65 us
    all_to_all x1 -> x2, blocking collectives: 23.5 us -> 23.5 us  [the longest x1 16.8 us: total_over_all(): lax.all_to_all(terms, 'mem', 0, 0).astype(F32)]
  transfers between devices with their start and end apart: 27 -> 24, of which waited for: 14 -> 17; matrix products, arithmetic and copies ran while one was open for 2% -> 2% of each run, Pallas kernels for 0% -> 0%
where the time goes in v1:
time: 139 us
  starting transfers between devices  34 us (24%)
  waiting for transfers between devices  33.6 us (24%)
  blocking collectives  31.3 us (23%)
  Pallas kernels  26.1 us (19%)
  between operations  6.55 us (5%)
  local copies, waits for them, and re-layouts  5.28 us (4%)
    ppermute x20, starting transfers between devices, passed_along(): return lax.ppermute(block, axis, route)  31.5 us
    pallas_call x6, Pallas kernels, step(): stage_call(stage.reshape(1), spacing_per_tier, *blocks, mixer_entry_proje...  25.1 us
    ppermute x20, waiting for transfers between devices, passed_along(): return lax.ppermute(block, axis, route)  21.4 us
    all_to_all x1, blocking collectives, total_over_all(): lax.all_to_all(terms, 'mem', 0, 0).astype(F32)  16.8 us
    ppermute x4, waiting for transfers between devices, total_over_all(): other = lax.ppermute(total, axis, list(enumerate(partner)))  12.3 us
    all_gather x1, blocking collectives, total_over_all(): full = lax.all_gather(total, 'core').reshape(2 * size.each, size.chans)  7.78 us
    all_to_all x1, blocking collectives, total_over_all(): lax.all_to_all(terms, 'core', 0, 0).astype(F32)  6.69 us
  transfers between devices with their start and end apart: 24, of which 17 were waited for; matrix products, arithmetic and copies ran while one was open for 2% of the time, Pallas kernels for 0%

profile of v1, /device:TPU:1, one launch (start us, length us, event | category | flops | bytes accessed | tf_op | source)
XLA Modules:
  0.0 138.7 jit_solution(14085997193556155118)
XLA Ops:
  0.6 1.4 fusion
  7.8 1.0 begin.1
  8.9 0.6 copy-done.2
  9.5 81.0 %while.45 = (s32[]{:T(128)}, bf16[384,128]{1,0:T(8,128)(2,1)S(1)}, f32[384,128]{1,0:T(8,128)S(1)}, bf16[2,384,128]{2,1,0:T(8,128)(2,1)S(1)}, bf16[2,384,128]{2,1...) while((s32[]{:T(128)}, bf16[384,128]{1,0:T(8,128)(2,1)S(1)}, ...), condition=%wide.region_5.0_spmd, body=%wide.region_0.0_spmd.sunk | while | flops 5 | bytes 3146185 | solution.py:386
  9.5 6.7 %conditional.2 = (bf16[384,128]{1,0:T(8,128)(2,1)}, bf16[384,128]{1,0:T(8,128)(2,1)}, bf16[384,128]{1,0:T(8,128)(2,1)}, bf16[384,128]{1,0:T(8,128)(2,1)}) conditional(s32[]{:T(128)} %clamp.8, bf16[384,128]{1,0:T(8,128)(2,1)S(1)} %get-tuple-element.511.field_in, ...), branch_computations={%region_1.0_spmd, %region_2.0_spmd, %region_3.0_spmd, %region_4.0_... | conditional | bytes 1573056 | solution.py:49
  9.5 2.6 %collective-permute-start = (bf16[384,128]{1,0:T(8,128)(2,1)S(1)}, bf16[384,128]{1,0:T(8,128)(2,1)}, u32[]{:S(2)}, u32[]{:S(2)}) collective-permute-start(bf16[384,128]{1,0:T(8,128)(2,1)S(1)} %param), channel_id=1, source_target_pairs={{248,0},{0,8},{8,16},{16,24},{24,32},{32,40},{40,48},{48,56},{56,6... | collective-permute-start | bytes 294920 | tf_op jit(solution)/shard_map/while/body/eval_jaxpr/cond/branch_0_fun/ppermute | solution.py:23
  12.1 0.6 collective-permute-start.1
  12.7 0.6 copy.27
  13.4 0.6 copy.28
  14.0 2.3 %collective-permute-done.1 = bf16[384,128]{1,0:T(8,128)(2,1)} collective-permute-done((bf16[384,128]{1,0:T(8,128)(2,1)S(1)}, bf16[384,128]{1,0:T(8,128)(2,1)}, u32[]{:S(2)}, u32[]{:S(2)}) %collective-permute-start.1) | collective-permute-done | bytes 98336 | tf_op jit(solution)/shard_map/while/body/eval_jaxpr/cond/branch_0_fun/ppermute | solution.py:23
  16.3 4.3 %stage.5 = (bf16[384,128]{1,0:T(8,128)(2,1)S(1)}, f32[384,128]{1,0:T(8,128)S(1)}, bf16[2,384,128]{2,1,0:T(8,128)(2,1)S(1)}, bf16[2,384,128]{2,1,0:T(8,128)(2,1)S...) custom-call(s32[1]{0:T(128)} %bitcast.18.stage_ref, ...), custom_call_target="tpu_custom_call", output_to_operand_aliasing={{0}: (10, {}), {1}: (11, {}), {2}: (12, {}), {3}: (13, {}),... | custom-call | tf_op jit(solution)/shard_map/while/body/eval_jaxpr/stage/pallas_call | solution.py:373
  20.7 11.5 %conditional.2 = (bf16[384,128]{1,0:T(8,128)(2,1)}, bf16[384,128]{1,0:T(8,128)(2,1)}, bf16[384,128]{1,0:T(8,128)(2,1)}, bf16[384,128]{1,0:T(8,128)(2,1)}) conditional(s32[]{:T(128)} %clamp.8, bf16[384,128]{1,0:T(8,128)(2,1)S(1)} %get-tuple-element.511.field_in, ...), branch_computations={%region_1.0_spmd, %region_2.0_spmd, %region_3.0_spmd, %region_4.0_... | conditional | bytes 1573056 | solution.py:49
  20.7 1.9 %collective-permute-start.10 = (bf16[384,128]{1,0:T(8,128)(2,1)S(1)}, bf16[384,128]{1,0:T(8,128)(2,1)}, u32[]{:S(2)}, u32[]{:S(2)}) collective-permute-start(bf16[384,128]{1,0:T(8,128)(2,1)S(1)} %param.3), channel_id=1, source_target_pairs={{224,0},{232,8},{240,16},{248,24},{0,32},{8,40},{16,48},{24,56},{3... | collective-permute-start | bytes 294920 | tf_op jit(solution)/shard_map/while/body/eval_jaxpr/cond/branch_3_fun/ppermute | solution.py:23
  22.6 1.5 %collective-permute-start.11 = (bf16[384,128]{1,0:T(8,128)(2,1)S(1)}, bf16[384,128]{1,0:T(8,128)(2,1)}, u32[]{:S(2)}, u32[]{:S(2)}) collective-permute-start(bf16[384,128]{1,0:T(8,128)(2,1)S(1)} %param.3), channel_id=1, source_target_pairs={{232,0},{240,8},{248,16},{0,24},{8,32},{16,40},{24,48},{32,56},{40... | collective-permute-start | bytes 294920 | tf_op jit(solution)/shard_map/while/body/eval_jaxpr/cond/branch_3_fun/ppermute | solution.py:23
  24.0 2.4 %collective-permute-start.12 = (bf16[384,128]{1,0:T(8,128)(2,1)S(1)}, bf16[384,128]{1,0:T(8,128)(2,1)}, u32[]{:S(2)}, u32[]{:S(2)}) collective-permute-start(bf16[384,128]{1,0:T(8,128)(2,1)S(1)} %param.3), channel_id=1, source_target_pairs={{24,0},{32,8},{40,16},{48,24},{56,32},{64,40},{72,48},{80,56},{88,... | collective-permute-start | bytes 294920 | tf_op jit(solution)/shard_map/while/body/eval_jaxpr/cond/branch_3_fun/ppermute | solution.py:23
  26.4 2.8 %collective-permute-start.13 = (bf16[384,128]{1,0:T(8,128)(2,1)S(1)}, bf16[384,128]{1,0:T(8,128)(2,1)}, u32[]{:S(2)}, u32[]{:S(2)}) collective-permute-start(bf16[384,128]{1,0:T(8,128)(2,1)S(1)} %param.3), channel_id=1, source_target_pairs={{32,0},{40,8},{48,16},{56,24},{64,32},{72,40},{80,48},{88,56},{96,... | collective-permute-start | bytes 294920 | tf_op jit(solution)/shard_map/while/body/eval_jaxpr/cond/branch_3_fun/ppermute | solution.py:23
  29.2 1.1 collective-permute-done.11
  30.4 0.2 collective-permute-done.12
  30.6 1.6 %collective-permute-done.13 = bf16[384,128]{1,0:T(8,128)(2,1)} collective-permute-done((bf16[384,128]{1,0:T(8,128)(2,1)S(1)}, bf16[384,128]{1,0:T(8,128)(2,1)}, u32[]{:S(2)}, u32[]{:S(2)}) %collective-permute-start.13) | collective-permute-done | bytes 98336 | tf_op jit(solution)/shard_map/while/body/eval_jaxpr/cond/branch_3_fun/ppermute | solution.py:23
  32.1 4.3 %stage.5 = (bf16[384,128]{1,0:T(8,128)(2,1)S(1)}, f32[384,128]{1,0:T(8,128)S(1)}, bf16[2,384,128]{2,1,0:T(8,128)(2,1)S(1)}, bf16[2,384,128]{2,1,0:T(8,128)(2,1)S...) custom-call(s32[1]{0:T(128)} %bitcast.18.stage_ref, ...), custom_call_target="tpu_custom_call", output_to_operand_aliasing={{0}: (10, {}), {1}: (11, {}), {2}: (12, {}), {3}: (13, {}),... | custom-call | tf_op jit(solution)/shard_map/while/body/eval_jaxpr/stage/pallas_call | solution.py:373
  36.5 12.4 %conditional.2 = (bf16[384,128]{1,0:T(8,128)(2,1)}, bf16[384,128]{1,0:T(8,128)(2,1)}, bf16[384,128]{1,0:T(8,128)(2,1)}, bf16[384,128]{1,0:T(8,128)(2,1)}) conditional(s32[]{:T(128)} %clamp.8, bf16[384,128]{1,0:T(8,128)(2,1)S(1)} %get-tuple-element.511.field_in, ...), branch_computations={%region_1.0_spmd, %region_2.0_spmd, %region_3.0_spmd, %region_4.0_... | conditional | bytes 1573056 | solution.py:49
  36.5 3.6 %collective-permute-start.6 = (bf16[384,128]{1,0:T(8,128)(2,1)S(1)}, bf16[384,128]{1,0:T(8,128)(2,1)}, u32[]{:S(2)}, u32[]{:S(2)}) collective-permute-start(bf16[384,128]{1,0:T(8,128)(2,1)S(1)} %param.2), channel_id=1, source_target_pairs={{232,0},{240,8},{248,16},{0,24},{8,32},{16,40},{24,48},{32,56},{40... | collective-permute-start | bytes 294920 | tf_op jit(solution)/shard_map/while/body/eval_jaxpr/cond/branch_2_fun/ppermute | solution.py:23
  40.1 0.5 collective-permute-start.7
  40.6 3.1 %collective-permute-start.8 = (bf16[384,128]{1,0:T(8,128)(2,1)S(1)}, bf16[384,128]{1,0:T(8,128)(2,1)}, u32[]{:S(2)}, u32[]{:S(2)}) collective-permute-start(bf16[384,128]{1,0:T(8,128)(2,1)S(1)} %param.2), channel_id=1, source_target_pairs={{16,0},{24,8},{32,16},{40,24},{48,32},{56,40},{64,48},{72,56},{80,... | collective-permute-start | bytes 294920 | tf_op jit(solution)/shard_map/while/body/eval_jaxpr/cond/branch_2_fun/ppermute | solution.py:23
  43.7 2.2 %collective-permute-done.7 = bf16[384,128]{1,0:T(8,128)(2,1)} collective-permute-done((bf16[384,128]{1,0:T(8,128)(2,1)S(1)}, bf16[384,128]{1,0:T(8,128)(2,1)}, u32[]{:S(2)}, u32[]{:S(2)}) %collective-permute-start.7) | collective-permute-done | bytes 98336 | tf_op jit(solution)/shard_map/while/body/eval_jaxpr/cond/branch_2_fun/ppermute | solution.py:23
  45.9 1.6 %collective-permute-done.8 = bf16[384,128]{1,0:T(8,128)(2,1)} collective-permute-done((bf16[384,128]{1,0:T(8,128)(2,1)S(1)}, bf16[384,128]{1,0:T(8,128)(2,1)}, u32[]{:S(2)}, u32[]{:S(2)}) %collective-permute-start.8) | collective-permute-done | bytes 98336 | tf_op jit(solution)/shard_map/while/body/eval_jaxpr/cond/branch_2_fun/ppermute | solution.py:23
  47.6 1.4 collective-permute-done.9
  48.9 5.0 %stage.5 = (bf16[384,128]{1,0:T(8,128)(2,1)S(1)}, f32[384,128]{1,0:T(8,128)S(1)}, bf16[2,384,128]{2,1,0:T(8,128)(2,1)S(1)}, bf16[2,384,128]{2,1,0:T(8,128)(2,1)S...) custom-call(s32[1]{0:T(128)} %bitcast.18.stage_ref, ...), custom_call_target="tpu_custom_call", output_to_operand_aliasing={{0}: (10, {}), {1}: (11, {}), {2}: (12, {}), {3}: (13, {}),... | custom-call | tf_op jit(solution)/shard_map/while/body/eval_jaxpr/stage/pallas_call | solution.py:373
  54.0 11.0 %conditional.2 = (bf16[384,128]{1,0:T(8,128)(2,1)}, bf16[384,128]{1,0:T(8,128)(2,1)}, bf16[384,128]{1,0:T(8,128)(2,1)}, bf16[384,128]{1,0:T(8,128)(2,1)}) conditional(s32[]{:T(128)} %clamp.8, bf16[384,128]{1,0:T(8,128)(2,1)S(1)} %get-tuple-element.511.field_in, ...), branch_computations={%region_1.0_spmd, %region_2.0_spmd, %region_3.0_spmd, %region_4.0_... | conditional | bytes 1573056 | solution.py:49
  54.0 1.6 %collective-permute-start.6 = (bf16[384,128]{1,0:T(8,128)(2,1)S(1)}, bf16[384,128]{1,0:T(8,128)(2,1)}, u32[]{:S(2)}, u32[]{:S(2)}) collective-permute-start(bf16[384,128]{1,0:T(8,128)(2,1)S(1)} %param.2), channel_id=1, source_target_pairs={{232,0},{240,8},{248,16},{0,24},{8,32},{16,40},{24,48},{32,56},{40... | collective-permute-start | bytes 294920 | tf_op jit(solution)/shard_map/while/body/eval_jaxpr/cond/branch_2_fun/ppermute | solution.py:23
  55.6 1.7 %collective-permute-start.7 = (bf16[384,128]{1,0:T(8,128)(2,1)S(1)}, bf16[384,128]{1,0:T(8,128)(2,1)}, u32[]{:S(2)}, u32[]{:S(2)}) collective-permute-start(bf16[384,128]{1,0:T(8,128)(2,1)S(1)} %param.2), channel_id=1, source_target_pairs={{240,0},{248,8},{0,16},{8,24},{16,32},{24,40},{32,48},{40,56},{48,... | collective-permute-start | bytes 294920 | tf_op jit(solution)/shard_map/while/body/eval_jaxpr/cond/branch_2_fun/ppermute | solution.py:23
  57.3 1.9 %collective-permute-start.8 = (bf16[384,128]{1,0:T(8,128)(2,1)S(1)}, bf16[384,128]{1,0:T(8,128)(2,1)}, u32[]{:S(2)}, u32[]{:S(2)}) collective-permute-start(bf16[384,128]{1,0:T(8,128)(2,1)S(1)} %param.2), channel_id=1, source_target_pairs={{16,0},{24,8},{32,16},{40,24},{48,32},{56,40},{64,48},{72,56},{80,... | collective-permute-start | bytes 294920 | tf_op jit(solution)/shard_map/while/body/eval_jaxpr/cond/branch_2_fun/ppermute | solution.py:23
  59.2 0.8 collective-permute-start.9
  60.0 1.3 collective-permute-done.6
  61.2 2.4 %collective-permute-done.7 = bf16[384,128]{1,0:T(8,128)(2,1)} collective-permute-done((bf16[384,128]{1,0:T(8,128)(2,1)S(1)}, bf16[384,128]{1,0:T(8,128)(2,1)}, u32[]{:S(2)}, u32[]{:S(2)}) %collective-permute-start.7) | collective-permute-done | bytes 98336 | tf_op jit(solution)/shard_map/while/body/eval_jaxpr/cond/branch_2_fun/ppermute | solution.py:23
  63.6 1.3 collective-permute-done.8
  64.9 4.2 %stage.5 = (bf16[384,128]{1,0:T(8,128)(2,1)S(1)}, f32[384,128]{1,0:T(8,128)S(1)}, bf16[2,384,128]{2,1,0:T(8,128)(2,1)S(1)}, bf16[2,384,128]{2,1,0:T(8,128)(2,1)S...) custom-call(s32[1]{0:T(128)} %bitcast.18.stage_ref, ...), custom_call_target="tpu_custom_call", output_to_operand_aliasing={{0}: (10, {}), {1}: (11, {}), {2}: (12, {}), {3}: (13, {}),... | custom-call | tf_op jit(solution)/shard_map/while/body/eval_jaxpr/stage/pallas_call | solution.py:373
  69.2 9.2 %conditional.2 = (bf16[384,128]{1,0:T(8,128)(2,1)}, bf16[384,128]{1,0:T(8,128)(2,1)}, bf16[384,128]{1,0:T(8,128)(2,1)}, bf16[384,128]{1,0:T(8,128)(2,1)}) conditional(s32[]{:T(128)} %clamp.8, bf16[384,128]{1,0:T(8,128)(2,1)S(1)} %get-tuple-element.511.field_in, ...), branch_computations={%region_1.0_spmd, %region_2.0_spmd, %region_3.0_spmd, %region_4.0_... | conditional | bytes 1573056 | solution.py:49
  69.3 0.7 collective-permute-start.10
  70.0 2.1 %collective-permute-start.11 = (bf16[384,128]{1,0:T(8,128)(2,1)S(1)}, bf16[384,128]{1,0:T(8,128)(2,1)}, u32[]{:S(2)}, u32[]{:S(2)}) collective-permute-start(bf16[384,128]{1,0:T(8,128)(2,1)S(1)} %param.3), channel_id=1, source_target_pairs={{232,0},{240,8},{248,16},{0,24},{8,32},{16,40},{24,48},{32,56},{40... | collective-permute-start | bytes 294920 | tf_op jit(solution)/shard_map/while/body/eval_jaxpr/cond/branch_3_fun/ppermute | solution.py:23
  72.0 1.8 %collective-permute-start.12 = (bf16[384,128]{1,0:T(8,128)(2,1)S(1)}, bf16[384,128]{1,0:T(8,128)(2,1)}, u32[]{:S(2)}, u32[]{:S(2)}) collective-permute-start(bf16[384,128]{1,0:T(8,128)(2,1)S(1)} %param.3), channel_id=1, source_target_pairs={{24,0},{32,8},{40,16},{48,24},{56,32},{64,40},{72,48},{80,56},{88,... | collective-permute-start | bytes 294920 | tf_op jit(solution)/shard_map/while/body/eval_jaxpr/cond/branch_3_fun/ppermute | solution.py:23
  73.8 0.8 collective-permute-start.13
  74.7 2.7 %collective-permute-done.11 = bf16[384,128]{1,0:T(8,128)(2,1)} collective-permute-done((bf16[384,128]{1,0:T(8,128)(2,1)S(1)}, bf16[384,128]{1,0:T(8,128)(2,1)}, u32[]{:S(2)}, u32[]{:S(2)}) %collective-permute-start.11) | collective-permute-done | bytes 98336 | tf_op jit(solution)/shard_map/while/body/eval_jaxpr/cond/branch_3_fun/ppermute | solution.py:23
  77.4 1.0 collective-permute-done.13
  78.4 4.2 %stage.5 = (bf16[384,128]{1,0:T(8,128)(2,1)S(1)}, f32[384,128]{1,0:T(8,128)S(1)}, bf16[2,384,128]{2,1,0:T(8,128)(2,1)S(1)}, bf16[2,384,128]{2,1,0:T(8,128)(2,1)S...) custom-call(s32[1]{0:T(128)} %bitcast.18.stage_ref, ...), custom_call_target="tpu_custom_call", output_to_operand_aliasing={{0}: (10, {}), {1}: (11, {}), {2}: (12, {}), {3}: (13, {}),... | custom-call | tf_op jit(solution)/shard_map/while/body/eval_jaxpr/stage/pallas_call | solution.py:373
  82.7 4.8 %conditional.2 = (bf16[384,128]{1,0:T(8,128)(2,1)}, bf16[384,128]{1,0:T(8,128)(2,1)}, bf16[384,128]{1,0:T(8,128)(2,1)}, bf16[384,128]{1,0:T(8,128)(2,1)}) conditional(s32[]{:T(128)} %clamp.8, bf16[384,128]{1,0:T(8,128)(2,1)S(1)} %get-tuple-element.511.field_in, ...), branch_computations={%region_1.0_spmd, %region_2.0_spmd, %region_3.0_spmd, %region_4.0_... | conditional | bytes 1573056 | solution.py:49
  82.7 0.6 collective-permute-start
  83.3 0.6 collective-permute-start.1
  83.9 0.6 copy.27
  84.5 0.6 copy.28
  85.2 2.3 %collective-permute-done.1 = bf16[384,128]{1,0:T(8,128)(2,1)} collective-permute-done((bf16[384,128]{1,0:T(8,128)(2,1)S(1)}, bf16[384,128]{1,0:T(8,128)(2,1)}, u32[]{:S(2)}, u32[]{:S(2)}) %collective-permute-start.1) | collective-permute-done | bytes 98336 | tf_op jit(solution)/shard_map/while/body/eval_jaxpr/cond/branch_0_fun/ppermute | solution.py:23
  87.5 2.9 %stage.5 = (bf16[384,128]{1,0:T(8,128)(2,1)S(1)}, f32[384,128]{1,0:T(8,128)S(1)}, bf16[2,384,128]{2,1,0:T(8,128)(2,1)S(1)}, bf16[2,384,128]{2,1,0:T(8,128)(2,1)S...) custom-call(s32[1]{0:T(128)} %bitcast.18.stage_ref, ...), custom_call_target="tpu_custom_call", output_to_operand_aliasing={{0}: (10, {}), {1}: (11, {}), {2}: (12, {}), {3}: (13, {}),... | custom-call | tf_op jit(solution)/shard_map/while/body/eval_jaxpr/stage/pallas_call | solution.py:373
  90.6 6.7 %all_to_all.10 = bf16[2,1792,128]{2,1,0:T(8,128)(2,1)S(1)} all-to-all(bf16[2,1792,128]{2,1,0:T(8,128)(2,1)S(1)} %bitcast.20), channel_id=1, replica_groups=mesh['z'=8,'xl'=2,'core'=2,'mem'=8] {'core'}, dimensions={0} | all-to-all | bytes 1835008 | tf_op jit(solution)/shard_map/all_to_all | solution.py:280
  97.3 0.4 reduce_sum.24
  97.7 16.8 %all_to_all.11 = bf16[8,224,128]{2,1,0:T(8,128)(2,1)S(1)} all-to-all(bf16[8,224,128]{2,1,0:T(8,128)(2,1)S(1)} %bitcast.22), channel_id=1, replica_groups=mesh['z'=8,'xl'=2,'core'=2,'mem'=8] {'mem'}, dimensions={0} | all-to-all | bytes 917504 | tf_op jit(solution)/shard_map/all_to_all | solution.py:282
  114.6 0.1 collective-permute-start.14
  114.7 3.0 %collective-permute-done.14 = bf16[224,128]{1,0:T(8,128)(2,1)S(1)} collective-permute-done((bf16[224,128]{1,0:T(8,128)(2,1)S(1)}, bf16[224,128]{1,0:T(8,128)(2,1)S(1)}, u32[]{:S(2)}, u32[]{:S(2)}) %collective-permute-start.14) | collective-permute-done | bytes 57376 | tf_op jit(solution)/shard_map/ppermute | solution.py:288
  117.8 3.0 %collective-permute-done.15 = bf16[224,128]{1,0:T(8,128)(2,1)S(1)} collective-permute-done((bf16[224,128]{1,0:T(8,128)(2,1)S(1)}, bf16[224,128]{1,0:T(8,128)(2,1)S(1)}, u32[]{:S(2)}, u32[]{:S(2)}) %collective-permute-start.15) | collective-permute-done | bytes 57376 | tf_op jit(solution)/shard_map/ppermute | solution.py:288
  121.0 4.2 %collective-permute-done.16 = bf16[224,128]{1,0:T(8,128)(2,1)S(1)} collective-permute-done((bf16[224,128]{1,0:T(8,128)(2,1)S(1)}, bf16[224,128]{1,0:T(8,128)(2,1)S(1)}, u32[]{:S(2)}, u32[]{:S(2)}) %collective-permute-start.16) | collective-permute-done | bytes 57376 | tf_op jit(solution)/shard_map/ppermute | solution.py:288
  125.2 2.2 %collective-permute-start.17 = (bf16[224,128]{1,0:T(8,128)(2,1)S(1)}, bf16[224,128]{1,0:T(8,128)(2,1)S(1)}, u32[]{:S(2)}, u32[]{:S(2)}) collective-permute-start(bf16[224,128]{1,0:T(8,128)(2,1)S(1)} %add_convert_fusion.1), channel_id=1, source_target_pairs={{0,224},{32,192},{64,160},{96,128},{128,96},{160,64},{192,32},{224... | collective-permute-start | bytes 172040 | tf_op jit(solution)/shard_map/ppermute | solution.py:288
  127.5 0.7 copy_bitcast_fusion
  128.2 2.0 %collective-permute-done.17 = bf16[224,128]{1,0:T(8,128)(2,1)S(1)} collective-permute-done((bf16[224,128]{1,0:T(8,128)(2,1)S(1)}, bf16[224,128]{1,0:T(8,128)(2,1)S(1)}, u32[]{:S(2)}, u32[]{:S(2)}) %collective-permute-start.17) | collective-permute-done | bytes 57376 | tf_op jit(solution)/shard_map/ppermute | solution.py:288
  130.2 7.8 %all-gather = bf16[448,128]{1,0:T(8,128)(2,1)S(1)} all-gather(bf16[224,128]{1,0:T(8,128)(2,1)S(1)} %add_convert_fusion), channel_id=2, replica_groups=mesh['z'=8,'xl'=2,'core'=2,'mem'=8] {'core'}, dimensions={0}, use_global_device_ids=true | all-gather | bytes 172032 | tf_op jit(solution)/shard_map/all_gather | solution.py:290
  138.0 0.7 convert_multiply_fusion
  (30 shorter events, 0.4 us)
Async XLA Ops:
  7.8 1.1 copy-start.1
  8.9 0.7 copy-start.2
  9.5 6.7 %copy-start = (bf16[3,128,512]{2,1,0:T(8,128)(2,1)S(1)}, bf16[3,128,512]{2,1,0:T(8,128)(2,1)}, u32[]{:S(2)}) copy-start(bf16[3,128,512]{2,1,0:T(8,128)(2,1)} %get-tuple-element.546.entry) | copy-start | bytes 1179652 | tf_op jit(solution)/shard_map/while
  9.5 4.5 %collective-permute-start = (bf16[384,128]{1,0:T(8,128)(2,1)S(1)}, bf16[384,128]{1,0:T(8,128)(2,1)}, u32[]{:S(2)}, u32[]{:S(2)}) collective-permute-start(bf16[384,128]{1,0:T(8,128)(2,1)S(1)} %param), channel_id=1, source_target_pairs={{248,0},{0,8},{8,16},{16,24},{24,32},{32,40},{40,48},{48,56},{56,6... | collective-permute-start | bytes 294920 | tf_op jit(solution)/shard_map/while/body/eval_jaxpr/cond/branch_0_fun/ppermute | solution.py:23
  12.1 4.1 %collective-permute-start.1 = (bf16[384,128]{1,0:T(8,128)(2,1)S(1)}, bf16[384,128]{1,0:T(8,128)(2,1)}, u32[]{:S(2)}, u32[]{:S(2)}) collective-permute-start(bf16[384,128]{1,0:T(8,128)(2,1)S(1)} %param), channel_id=1, source_target_pairs={{8,0},{16,8},{24,16},{32,24},{40,32},{48,40},{56,48},{64,56},{72,6... | collective-permute-start | bytes 294920 | tf_op jit(solution)/shard_map/while/body/eval_jaxpr/cond/branch_0_fun/ppermute | solution.py:23
  20.6 11.5 %copy-start = (bf16[3,128,512]{2,1,0:T(8,128)(2,1)S(1)}, bf16[3,128,512]{2,1,0:T(8,128)(2,1)}, u32[]{:S(2)}) copy-start(bf16[3,128,512]{2,1,0:T(8,128)(2,1)} %get-tuple-element.546.entry) | copy-start | bytes 1179652 | tf_op jit(solution)/shard_map/while
  20.7 8.6 %collective-permute-start.10 = (bf16[384,128]{1,0:T(8,128)(2,1)S(1)}, bf16[384,128]{1,0:T(8,128)(2,1)}, u32[]{:S(2)}, u32[]{:S(2)}) collective-permute-start(bf16[384,128]{1,0:T(8,128)(2,1)S(1)} %param.3), channel_id=1, source_target_pairs={{224,0},{232,8},{240,16},{248,24},{0,32},{8,40},{16,48},{24,56},{3... | collective-permute-start | bytes 294920 | tf_op jit(solution)/shard_map/while/body/eval_jaxpr/cond/branch_3_fun/ppermute | solution.py:23
  22.6 7.8 %collective-permute-start.11 = (bf16[384,128]{1,0:T(8,128)(2,1)S(1)}, bf16[384,128]{1,0:T(8,128)(2,1)}, u32[]{:S(2)}, u32[]{:S(2)}) collective-permute-start(bf16[384,128]{1,0:T(8,128)(2,1)S(1)} %param.3), channel_id=1, source_target_pairs={{232,0},{240,8},{248,16},{0,24},{8,32},{16,40},{24,48},{32,56},{40... | collective-permute-start | bytes 294920 | tf_op jit(solution)/shard_map/while/body/eval_jaxpr/cond/branch_3_fun/ppermute | solution.py:23
  24.0 6.5 %collective-permute-start.12 = (bf16[384,128]{1,0:T(8,128)(2,1)S(1)}, bf16[384,128]{1,0:T(8,128)(2,1)}, u32[]{:S(2)}, u32[]{:S(2)}) collective-permute-start(bf16[384,128]{1,0:T(8,128)(2,1)S(1)} %param.3), channel_id=1, source_target_pairs={{24,0},{32,8},{40,16},{48,24},{56,32},{64,40},{72,48},{80,56},{88,... | collective-permute-start | bytes 294920 | tf_op jit(solution)/shard_map/while/body/eval_jaxpr/cond/branch_3_fun/ppermute | solution.py:23
  26.4 5.7 %collective-permute-start.13 = (bf16[384,128]{1,0:T(8,128)(2,1)S(1)}, bf16[384,128]{1,0:T(8,128)(2,1)}, u32[]{:S(2)}, u32[]{:S(2)}) collective-permute-start(bf16[384,128]{1,0:T(8,128)(2,1)S(1)} %param.3), channel_id=1, source_target_pairs={{32,0},{40,8},{48,16},{56,24},{64,32},{72,40},{80,48},{88,56},{96,... | collective-permute-start | bytes 294920 | tf_op jit(solution)/shard_map/while/body/eval_jaxpr/cond/branch_3_fun/ppermute | solution.py:23
  36.5 12.4 %copy-start = (bf16[3,128,512]{2,1,0:T(8,128)(2,1)S(1)}, bf16[3,128,512]{2,1,0:T(8,128)(2,1)}, u32[]{:S(2)}) copy-start(bf16[3,128,512]{2,1,0:T(8,128)(2,1)} %get-tuple-element.546.entry) | copy-start | bytes 1179652 | tf_op jit(solution)/shard_map/while
  36.5 7.2 %collective-permute-start.6 = (bf16[384,128]{1,0:T(8,128)(2,1)S(1)}, bf16[384,128]{1,0:T(8,128)(2,1)}, u32[]{:S(2)}, u32[]{:S(2)}) collective-permute-start(bf16[384,128]{1,0:T(8,128)(2,1)S(1)} %param.2), channel_id=1, source_target_pairs={{232,0},{240,8},{248,16},{0,24},{8,32},{16,40},{24,48},{32,56},{40... | collective-permute-start | bytes 294920 | tf_op jit(solution)/shard_map/while/body/eval_jaxpr/cond/branch_2_fun/ppermute | solution.py:23
  40.1 5.8 %collective-permute-start.7 = (bf16[384,128]{1,0:T(8,128)(2,1)S(1)}, bf16[384,128]{1,0:T(8,128)(2,1)}, u32[]{:S(2)}, u32[]{:S(2)}) collective-permute-start(bf16[384,128]{1,0:T(8,128)(2,1)S(1)} %param.2), channel_id=1, source_target_pairs={{240,0},{248,8},{0,16},{8,24},{16,32},{24,40},{32,48},{40,56},{48,... | collective-permute-start | bytes 294920 | tf_op jit(solution)/shard_map/while/body/eval_jaxpr/cond/branch_2_fun/ppermute | solution.py:23
  40.6 7.0 %collective-permute-start.8 = (bf16[384,128]{1,0:T(8,128)(2,1)S(1)}, bf16[384,128]{1,0:T(8,128)(2,1)}, u32[]{:S(2)}, u32[]{:S(2)}) collective-permute-start(bf16[384,128]{1,0:T(8,128)(2,1)S(1)} %param.2), channel_id=1, source_target_pairs={{16,0},{24,8},{32,16},{40,24},{48,32},{56,40},{64,48},{72,56},{80,... | collective-permute-start | bytes 294920 | tf_op jit(solution)/shard_map/while/body/eval_jaxpr/cond/branch_2_fun/ppermute | solution.py:23
  43.7 5.2 %collective-permute-start.9 = (bf16[384,128]{1,0:T(8,128)(2,1)S(1)}, bf16[384,128]{1,0:T(8,128)(2,1)}, u32[]{:S(2)}, u32[]{:S(2)}) collective-permute-start(bf16[384,128]{1,0:T(8,128)(2,1)S(1)} %param.2), channel_id=1, source_target_pairs={{24,0},{32,8},{40,16},{48,24},{56,32},{64,40},{72,48},{80,56},{88,... | collective-permute-start | bytes 294920 | tf_op jit(solution)/shard_map/while/body/eval_jaxpr/cond/branch_2_fun/ppermute | solution.py:23
  54.0 11.0 %copy-start = (bf16[3,128,512]{2,1,0:T(8,128)(2,1)S(1)}, bf16[3,128,512]{2,1,0:T(8,128)(2,1)}, u32[]{:S(2)}) copy-start(bf16[3,128,512]{2,1,0:T(8,128)(2,1)} %get-tuple-element.546.entry) | copy-start | bytes 1179652 | tf_op jit(solution)/shard_map/while
  54.0 7.2 %collective-permute-start.6 = (bf16[384,128]{1,0:T(8,128)(2,1)S(1)}, bf16[384,128]{1,0:T(8,128)(2,1)}, u32[]{:S(2)}, u32[]{:S(2)}) collective-permute-start(bf16[384,128]{1,0:T(8,128)(2,1)S(1)} %param.2), channel_id=1, source_target_pairs={{232,0},{240,8},{248,16},{0,24},{8,32},{16,40},{24,48},{32,56},{40... | collective-permute-start | bytes 294920 | tf_op jit(solution)/shard_map/while/body/eval_jaxpr/cond/branch_2_fun/ppermute | solution.py:23
  55.6 8.0 %collective-permute-start.7 = (bf16[384,128]{1,0:T(8,128)(2,1)S(1)}, bf16[384,128]{1,0:T(8,128)(2,1)}, u32[]{:S(2)}, u32[]{:S(2)}) collective-permute-start(bf16[384,128]{1,0:T(8,128)(2,1)S(1)} %param.2), channel_id=1, source_target_pairs={{240,0},{248,8},{0,16},{8,24},{16,32},{24,40},{32,48},{40,56},{48,... | collective-permute-start | bytes 294920 | tf_op jit(solution)/shard_map/while/body/eval_jaxpr/cond/branch_2_fun/ppermute | solution.py:23
  57.3 7.6 %collective-permute-start.8 = (bf16[384,128]{1,0:T(8,128)(2,1)S(1)}, bf16[384,128]{1,0:T(8,128)(2,1)}, u32[]{:S(2)}, u32[]{:S(2)}) collective-permute-start(bf16[384,128]{1,0:T(8,128)(2,1)S(1)} %param.2), channel_id=1, source_target_pairs={{16,0},{24,8},{32,16},{40,24},{48,32},{56,40},{64,48},{72,56},{80,... | collective-permute-start | bytes 294920 | tf_op jit(solution)/shard_map/while/body/eval_jaxpr/cond/branch_2_fun/ppermute | solution.py:23
  59.2 5.7 %collective-permute-start.9 = (bf16[384,128]{1,0:T(8,128)(2,1)S(1)}, bf16[384,128]{1,0:T(8,128)(2,1)}, u32[]{:S(2)}, u32[]{:S(2)}) collective-permute-start(bf16[384,128]{1,0:T(8,128)(2,1)S(1)} %param.2), channel_id=1, source_target_pairs={{24,0},{32,8},{40,16},{48,24},{56,32},{64,40},{72,48},{80,56},{88,... | collective-permute-start | bytes 294920 | tf_op jit(solution)/shard_map/while/body/eval_jaxpr/cond/branch_2_fun/ppermute | solution.py:23
  69.2 9.2 %copy-start = (bf16[3,128,512]{2,1,0:T(8,128)(2,1)S(1)}, bf16[3,128,512]{2,1,0:T(8,128)(2,1)}, u32[]{:S(2)}) copy-start(bf16[3,128,512]{2,1,0:T(8,128)(2,1)} %get-tuple-element.546.entry) | copy-start | bytes 1179652 | tf_op jit(solution)/shard_map/while
  69.3 5.4 %collective-permute-start.10 = (bf16[384,128]{1,0:T(8,128)(2,1)S(1)}, bf16[384,128]{1,0:T(8,128)(2,1)}, u32[]{:S(2)}, u32[]{:S(2)}) collective-permute-start(bf16[384,128]{1,0:T(8,128)(2,1)S(1)} %param.3), channel_id=1, source_target_pairs={{224,0},{232,8},{240,16},{248,24},{0,32},{8,40},{16,48},{24,56},{3... | collective-permute-start | bytes 294920 | tf_op jit(solution)/shard_map/while/body/eval_jaxpr/cond/branch_3_fun/ppermute | solution.py:23
  70.0 7.4 %collective-permute-start.11 = (bf16[384,128]{1,0:T(8,128)(2,1)S(1)}, bf16[384,128]{1,0:T(8,128)(2,1)}, u32[]{:S(2)}, u32[]{:S(2)}) collective-permute-start(bf16[384,128]{1,0:T(8,128)(2,1)S(1)} %param.3), channel_id=1, source_target_pairs={{232,0},{240,8},{248,16},{0,24},{8,32},{16,40},{24,48},{32,56},{40... | collective-permute-start | bytes 294920 | tf_op jit(solution)/shard_map/while/body/eval_jaxpr/cond/branch_3_fun/ppermute | solution.py:23
  72.0 5.3 %collective-permute-start.12 = (bf16[384,128]{1,0:T(8,128)(2,1)S(1)}, bf16[384,128]{1,0:T(8,128)(2,1)}, u32[]{:S(2)}, u32[]{:S(2)}) collective-permute-start(bf16[384,128]{1,0:T(8,128)(2,1)S(1)} %param.3), channel_id=1, source_target_pairs={{24,0},{32,8},{40,16},{48,24},{56,32},{64,40},{72,48},{80,56},{88,... | collective-permute-start | bytes 294920 | tf_op jit(solution)/shard_map/while/body/eval_jaxpr/cond/branch_3_fun/ppermute | solution.py:23
  73.8 4.6 %collective-permute-start.13 = (bf16[384,128]{1,0:T(8,128)(2,1)S(1)}, bf16[384,128]{1,0:T(8,128)(2,1)}, u32[]{:S(2)}, u32[]{:S(2)}) collective-permute-start(bf16[384,128]{1,0:T(8,128)(2,1)S(1)} %param.3), channel_id=1, source_target_pairs={{32,0},{40,8},{48,16},{56,24},{64,32},{72,40},{80,48},{88,56},{96,... | collective-permute-start | bytes 294920 | tf_op jit(solution)/shard_map/while/body/eval_jaxpr/cond/branch_3_fun/ppermute | solution.py:23
  82.6 4.8 %copy-start = (bf16[3,128,512]{2,1,0:T(8,128)(2,1)S(1)}, bf16[3,128,512]{2,1,0:T(8,128)(2,1)}, u32[]{:S(2)}) copy-start(bf16[3,128,512]{2,1,0:T(8,128)(2,1)} %get-tuple-element.546.entry) | copy-start | bytes 1179652 | tf_op jit(solution)/shard_map/while
  82.7 2.5 %collective-permute-start = (bf16[384,128]{1,0:T(8,128)(2,1)S(1)}, bf16[384,128]{1,0:T(8,128)(2,1)}, u32[]{:S(2)}, u32[]{:S(2)}) collective-permute-start(bf16[384,128]{1,0:T(8,128)(2,1)S(1)} %param), channel_id=1, source_target_pairs={{248,0},{0,8},{8,16},{16,24},{24,32},{32,40},{40,48},{48,56},{56,6... | collective-permute-start | bytes 294920 | tf_op jit(solution)/shard_map/while/body/eval_jaxpr/cond/branch_0_fun/ppermute | solution.py:23
  83.3 4.1 %collective-permute-start.1 = (bf16[384,128]{1,0:T(8,128)(2,1)S(1)}, bf16[384,128]{1,0:T(8,128)(2,1)}, u32[]{:S(2)}, u32[]{:S(2)}) collective-permute-start(bf16[384,128]{1,0:T(8,128)(2,1)S(1)} %param), channel_id=1, source_target_pairs={{8,0},{16,8},{24,16},{32,24},{40,32},{48,40},{56,48},{64,56},{72,6... | collective-permute-start | bytes 294920 | tf_op jit(solution)/shard_map/while/body/eval_jaxpr/cond/branch_0_fun/ppermute | solution.py:23
  114.6 3.1 %collective-permute-start.14 = (bf16[224,128]{1,0:T(8,128)(2,1)S(1)}, bf16[224,128]{1,0:T(8,128)(2,1)S(1)}, u32[]{:S(2)}, u32[]{:S(2)}) collective-permute-start(bf16[224,128]{1,0:T(8,128)(2,1)S(1)} %reduce_sum.25), channel_id=1, source_target_pairs={{0,16},{16,0},{1,17},{17,1},{2,18},{18,2},{3,19},{19,3},{4,20},{20... | collective-permute-start | bytes 172040 | tf_op jit(solution)/shard_map/ppermute | solution.py:288
  117.7 3.1 %collective-permute-start.15 = (bf16[224,128]{1,0:T(8,128)(2,1)S(1)}, bf16[224,128]{1,0:T(8,128)(2,1)S(1)}, u32[]{:S(2)}, u32[]{:S(2)}) collective-permute-start(bf16[224,128]{1,0:T(8,128)(2,1)S(1)} %add_convert_fusion.3), channel_id=1, source_target_pairs={{0,32},{32,0},{64,96},{96,64},{128,160},{160,128},{192,224},{224,1... | collective-permute-start | bytes 172040 | tf_op jit(solution)/shard_map/ppermute | solution.py:288
  120.9 4.4 %collective-permute-start.16 = (bf16[224,128]{1,0:T(8,128)(2,1)S(1)}, bf16[224,128]{1,0:T(8,128)(2,1)S(1)}, u32[]{:S(2)}, u32[]{:S(2)}) collective-permute-start(bf16[224,128]{1,0:T(8,128)(2,1)S(1)} %add_convert_fusion.2), channel_id=1, source_target_pairs={{0,64},{32,96},{64,0},{96,32},{128,192},{160,224},{192,128},{224,1... | collective-permute-start | bytes 172040 | tf_op jit(solution)/shard_map/ppermute | solution.py:288
  125.2 4.9 %collective-permute-start.17 = (bf16[224,128]{1,0:T(8,128)(2,1)S(1)}, bf16[224,128]{1,0:T(8,128)(2,1)S(1)}, u32[]{:S(2)}, u32[]{:S(2)}) collective-permute-start(bf16[224,128]{1,0:T(8,128)(2,1)S(1)} %add_convert_fusion.1), channel_id=1, source_target_pairs={{0,224},{32,192},{64,160},{96,128},{128,96},{160,64},{192,32},{224... | collective-permute-start | bytes 172040 | tf_op jit(solution)/shard_map/ppermute | solution.py:288

commit v2 on v1

--- a/solution.py
+++ b/solution.py
@@ -141,31 +141,38 @@
 
 
 def stage_body(
-    size, stage_ref, spacing_ref, fl, nl, nu, fu, entry, leave, cot, conv, field_in, grad_in, *refs
+    size, stage_ref, spacing_ref, cot, fl, nl, nu, fu, entries, leaves, conv, field_in, grad_in, *refs
 ):
     field, grad_out, hidden, mixed, pre_conv, lower, upper, terms, outcome, first = refs[8:18]
-    left, middle, right, back, kernel, own, narrow, pre, before, after, found, block, wide, sems = refs[18:]
+    left, middle, right, back, kernel, own, narrow, pre, before, after, found, block = refs[18:30]
+    wide, entry, leave, came_in, sems, more = refs[30:]
     stage = stage_ref[0]
     forward = stage < LAYERS
     turn = stage == LAYERS - 1
     final = stage == 2 * LAYERS - 1
     layer = jnp.where(forward, stage, 2 * LAYERS - 1 - stage)
     at = jnp.where(forward, stage, jnp.maximum(2 * LAYERS - 2 - stage, 0))
-    kept = jnp.minimum(at, LAYERS - 2)
     inner = pl.ds(size.pitch, size.cells)
-    pairs = (
-        (hidden, own.at[inner]), (mixed, narrow), (pre_conv, pre), (lower, before), (upper, after)
-    )
-    weights = pltpu.make_async_copy(conv.at[layer], kernel, sems.at[0])
+    blocks = [
+        pltpu.make_async_copy(there, came_in.at[i], more.at[i])
+        for i, there in enumerate((fl, nl, nu, fu))
+    ]
+    weights = [
+        pltpu.make_async_copy(conv.at[layer], kernel, sems.at[0]),
+        pltpu.make_async_copy(entries.at[at], entry, more.at[4]),
+        pltpu.make_async_copy(leaves.at[at], leave, more.at[5]),
+    ]
+    kept = (hidden, mixed, pre_conv, lower, upper)
     loads = [
-        pltpu.make_async_copy(there.at[kept], here, sems.at[1 + i])
-        for i, (there, here) in enumerate(pairs)
+        pltpu.make_async_copy(there.at[at], here, sems.at[1 + i])
+        for i, (there, here) in enumerate(zip(kept, (own.at[inner], narrow, pre, before, after)))
     ]
     saves = [
-        pltpu.make_async_copy(here, there.at[kept], sems.at[1 + i])
-        for i, (there, here) in enumerate(pairs)
+        pltpu.make_async_copy(here, there.at[at], sems.at[1 + i])
+        for i, (there, here) in enumerate(zip(kept, (middle.at[inner], narrow, pre, left, right)))
     ]
-    weights.start()
+    for copy in blocks + weights:
+        copy.start()
 
     @pl.when(~forward & ~final)
     def _():
@@ -175,31 +182,32 @@
     spacing = spacing_ref[layer]
     near = sum((spacing > hop * size.ncols).astype(jnp.int32) for hop in range(1, size.hops))
     shifted = (left, middle, right)
-    fill_shifted(size, spacing - near * size.ncols, (fl, nl, field_in[...], nu, fu), shifted)
-    weights.wait()
+    for copy in blocks:
+        copy.wait()
+    parts = (came_in.at[0], came_in.at[1], field_in[...], came_in.at[2], came_in.at[3])
+    fill_shifted(size, spacing - near * size.ncols, parts, shifted)
+    for copy in weights:
+        copy.wait()
 
     @pl.when(forward)
     def _():
+        for copy in (saves[0], saves[3], saves[4]):
+            copy.start()
         mine = middle[inner, :]
         taps = taps_of(size, shifted)
-        before[...] = left[...]
-        after[...] = right[...]
-        own[...] = middle[...]
         value = matmul(taps, kernel[...])
         total = mine.astype(F32) + silu(value)
         small = total.astype(BF16)
         pre[...] = value
         narrow[...] = small
-        act = silu(matmul(small, entry[at])).astype(BF16)
-        total = total + matmul(act, leave[at])
+        saves[1].start()
+        saves[2].start()
+        act = silu(matmul(small, entry[...])).astype(BF16)
+        total = total + matmul(act, leave[...])
 
         @pl.when(~turn)
         def _():
-            for copy in saves:
-                copy.start()
             field[...] = jnp.where(valid_cells(size), total, 0.0).astype(BF16)
-            for copy in saves:
-                copy.wait()
 
         @pl.when(turn)
         def _():
@@ -208,6 +216,12 @@
             copy.start()
             back[...] = jnp.zeros(back.shape, back.dtype)
             turned_into(size, wide, back, cot[...])
+            before[...] = left[...]
+            after[...] = right[...]
+            own[...] = middle[...]
+            copy.wait()
+
+        for copy in saves:
             copy.wait()
 
     @pl.when(~forward)
@@ -238,9 +252,9 @@
     @pl.when((stage >= LAYERS - 1) & ~final)
     def _():
         came = back[...]
-        pre_mlp = matmul(narrow[...], entry[at])
-        grad_pre = (matmul(came, leave[at], ((1,), (1,))) * slope(pre_mlp)).astype(BF16)
-        grad = came.astype(F32) + matmul(grad_pre, entry[at], ((1,), (1,)))
+        pre_mlp = matmul(narrow[...], entry[...])
+        grad_pre = (matmul(came, leave[...], ((1,), (1,))) * slope(pre_mlp)).astype(BF16)
+        grad = came.astype(F32) + matmul(grad_pre, entry[...], ((1,), (1,)))
         grad_out[...] = grad
         grad_conv = (grad * slope(pre[...])).astype(BF16)
         field[...] = grad_conv
@@ -273,6 +287,7 @@
 VMEM_SPEC = pl.BlockSpec(memory_space=pltpu.VMEM)
 SMEM_SPEC = pl.BlockSpec(memory_space=pltpu.SMEM)
 ANY_SPEC = pl.BlockSpec(memory_space=pl.ANY)
+HBM_SPEC = pl.BlockSpec(memory_space=pltpu.HBM)
 
 
 def total_over_all(size, terms):
@@ -319,11 +334,11 @@
     kinds = [
         array(*cells),
         array(*cells, dtype=F32),
-        array(LAYERS - 1, *cells),
-        array(LAYERS - 1, *cells),
-        array(LAYERS - 1, *cells, dtype=F32),
-        array(LAYERS - 1, *tall),
-        array(LAYERS - 1, *tall),
+        array(LAYERS, *cells),
+        array(LAYERS, *cells),
+        array(LAYERS, *cells, dtype=F32),
+        array(LAYERS, *tall),
+        array(LAYERS, *tall),
         array(2 * size.members * size.each, chans),
         array(rows, ncols, chans),
         array(rows, ncols, chans),
@@ -333,20 +348,18 @@
         functools.partial(begin_body, size),
         out_shape=kinds,
         in_specs=[VMEM_SPEC] * 2,
-        out_specs=[VMEM_SPEC] + [ANY_SPEC] * (held - 1),
+        out_specs=[VMEM_SPEC, ANY_SPEC] + [HBM_SPEC] * 5 + [ANY_SPEC] * 3,
         scratch_shapes=[pltpu.VMEM((rows * ncols, chans), F32)],
         name="begin",
     )(columns_first(assimilated_snapshot), columns_first(stochastic_displacement[0]))
-    near = [
-        sum((spacing_per_tier[i] > hop * ncols).astype(jnp.int32) for hop in range(1, size.hops))
-        for i in range(LAYERS)
-    ]
-    code = sum(n << (4 * i) for i, n in enumerate(near + near[::-1]))
-    state_specs = [VMEM_SPEC] * 2 + [ANY_SPEC] * (held - 2)
+    near = sum((spacing_per_tier > hop * ncols).astype(jnp.int32) for hop in range(1, size.hops))
+    order = jnp.arange(LAYERS)
+    code = jnp.sum(near * ((1 << (4 * order)) + (1 << (4 * (2 * LAYERS - 1 - order)))))
+    state_specs = [VMEM_SPEC] * 2 + [HBM_SPEC] * 5 + [ANY_SPEC] * 3
     stage_call = pl.pallas_call(
         functools.partial(stage_body, size),
         out_shape=kinds,
-        in_specs=[SMEM_SPEC] * 2 + [VMEM_SPEC] * 7 + [ANY_SPEC] + state_specs,
+        in_specs=[SMEM_SPEC] * 2 + [VMEM_SPEC] + [HBM_SPEC] * 7 + state_specs,
         out_specs=state_specs,
         scratch_shapes=[pltpu.VMEM(tall, BF16)] * 3
         + [
@@ -360,7 +373,11 @@
             pltpu.VMEM((9 * chans, chans), BF16),
             pltpu.VMEM((rows, ncols, chans), BF16),
             pltpu.VMEM((rows * ncols, chans), F32),
+            pltpu.VMEM((chans, size.hidden), BF16),
+            pltpu.VMEM((size.hidden, chans), BF16),
+            pltpu.VMEM((4, *cells), BF16),
             pltpu.SemaphoreType.DMA((7 + size.pieces,)),
+            pltpu.SemaphoreType.DMA((6,)),
         ],
         input_output_aliases={10 + i: i for i in range(held)},
         name="stage",
@@ -373,10 +390,10 @@
             *stage_call(
                 stage.reshape(1),
                 spacing_per_tier,
+                columns_first(outcome_cotangent_vector[0]),
                 *blocks,
                 mixer_entry_projection,
                 mixer_exit_projection,
-                columns_first(outcome_cotangent_vector[0]),
                 spatial_window_coefficients,
                 *state,
             ),

time: 139 us -> 146 us (1.050)
  loops' own time: 0.54 us -> 11.4 us
  between operations: 6.55 us -> 0.7 us
  Pallas kernels: 26.1 us -> 28.1 us
  starting transfers between devices: 34 us -> 35.5 us
    another operation x1, loops' own time: 0.39 us -> 11.2 us  [per_device(): state = lax.fori_loop(0, 2 * LAYERS, step, (*state, code))]
    pallas_call x6, Pallas kernels: 25.1 us -> 27.1 us  [step(): stage_call(stage.reshape(1), spacing_per_tier, columns_first(outcome_cota...]
    ppermute x20, starting transfers between devices: 31.5 us -> 33.5 us  [passed_along(): return lax.ppermute(block, axis, route)]
    ppermute x20, waiting for transfers between devices: 21.4 us -> 19.7 us  [passed_along(): return lax.ppermute(block, axis, route)]
  transfers between devices with their start and end apart: 24 -> 24, of which waited for: 17 -> 16; matrix products, arithmetic and copies ran while one was open for 2% -> 2% of each run, Pallas kernels for 0% -> 0%
where the time goes in v2:
time: 146 us
  starting transfers between devices  35.5 us (24%)
  waiting for transfers between devices  32.4 us (22%)
  blocking collectives  31.8 us (22%)
  Pallas kernels  28.1 us (19%)
  loops' own time  11.4 us (8%)
  local copies, waits for them, and re-layouts  3.98 us (3%)
  other arithmetic  1.92 us (1%)
    ppermute x20, starting transfers between devices, passed_along(): return lax.ppermute(block, axis, route)  33.5 us
    pallas_call x6, Pallas kernels, step(): stage_call(stage.reshape(1), spacing_per_tier, columns_first(outcome_cota...  27.1 us
    ppermute x20, waiting for transfers between devices, passed_along(): return lax.ppermute(block, axis, route)  19.7 us
    all_to_all x1, blocking collectives, total_over_all(): lax.all_to_all(terms, 'mem', 0, 0).astype(F32)  16.8 us
    ppermute x4, waiting for transfers between devices, total_over_all(): other = lax.ppermute(total, axis, list(enumerate(partner)))  12.7 us
    another operation x1, loops' own time, per_device(): state = lax.fori_loop(0, 2 * LAYERS, step, (*state, code))  11.2 us
    all_gather x1, blocking collectives, total_over_all(): full = lax.all_gather(total, 'core').reshape(2 * size.each, size.chans)  7.83 us
    all_to_all x1, blocking collectives, total_over_all(): lax.all_to_all(terms, 'core', 0, 0).astype(F32)  7.23 us
  transfers between devices with their start and end apart: 24, of which 16 were waited for; matrix products, arithmetic and copies ran while one was open for 2% of the time, Pallas kernels for 0%

profile of v2, /device:TPU:1, one launch (start us, length us, event | category | flops | bytes accessed | tf_op | source)
XLA Modules:
  0.0 145.9 jit_solution(4288456108536503575)
XLA Ops:
  0.6 0.6 copy-done.3
  1.3 0.6 fusion.5
  1.9 1.0 begin.1
  2.9 94.3 %while.45 = (s32[]{:T(128)}, bf16[384,128]{1,0:T(8,128)(2,1)S(1)}, f32[384,128]{1,0:T(8,128)S(1)}, bf16[3,384,128]{2,1,0:T(8,128)(2,1)S(1)}, bf16[3,384,128]{2,1...) while((s32[]{:T(128)}, bf16[384,128]{1,0:T(8,128)(2,1)S(1)}, ...), condition=%wide.region_6.0_spmd, body=%wide.region_1.0_spmd.sunk | while | flops 5 | bytes 3146185 | solution.py:403
  3.6 6.8 %conditional.2 = (bf16[384,128]{1,0:T(8,128)(2,1)}, bf16[384,128]{1,0:T(8,128)(2,1)}, bf16[384,128]{1,0:T(8,128)(2,1)}, bf16[384,128]{1,0:T(8,128)(2,1)}) conditional(s32[]{:T(128)} %clamp.8, bf16[384,128]{1,0:T(8,128)(2,1)S(1)} %get-tuple-element.508.field_in, ...), branch_computations={%region_2.0_spmd, %region_3.0_spmd, %region_4.0_spmd, %region_5.0_... | conditional | bytes 1573056 | solution.py:49
  3.7 2.7 %collective-permute-start = (bf16[384,128]{1,0:T(8,128)(2,1)S(1)}, bf16[384,128]{1,0:T(8,128)(2,1)}, u32[]{:S(2)}, u32[]{:S(2)}) collective-permute-start(bf16[384,128]{1,0:T(8,128)(2,1)S(1)} %param), channel_id=1, source_target_pairs={{248,0},{0,8},{8,16},{16,24},{24,32},{32,40},{40,48},{48,56},{56,6... | collective-permute-start | bytes 294920 | tf_op jit(solution)/shard_map/while/body/eval_jaxpr/cond/branch_0_fun/ppermute | solution.py:23
  6.3 0.7 collective-permute-start.1
  7.0 0.6 copy.27
  7.7 0.6 copy.28
  8.3 2.2 %collective-permute-done.1 = bf16[384,128]{1,0:T(8,128)(2,1)} collective-permute-done((bf16[384,128]{1,0:T(8,128)(2,1)S(1)}, bf16[384,128]{1,0:T(8,128)(2,1)}, u32[]{:S(2)}, u32[]{:S(2)}) %collective-permute-start.1) | collective-permute-done | bytes 98336 | tf_op jit(solution)/shard_map/while/body/eval_jaxpr/cond/branch_0_fun/ppermute | solution.py:23
  10.5 4.4 %stage.5 = (bf16[384,128]{1,0:T(8,128)(2,1)S(1)}, f32[384,128]{1,0:T(8,128)S(1)}, bf16[3,384,128]{2,1,0:T(8,128)(2,1)S(1)}, bf16[3,384,128]{2,1,0:T(8,128)(2,1)S...) custom-call(s32[1]{0:T(128)} %bitcast.17.stage_ref, ...), custom_call_target="tpu_custom_call", output_to_operand_aliasing={{0}: (10, {}), {1}: (11, {}), {2}: (12, {}), {3}: (13, {}),... | custom-call | tf_op jit(solution)/shard_map/while/body/eval_jaxpr/stage/pallas_call | solution.py:390
  16.8 11.7 %conditional.2 = (bf16[384,128]{1,0:T(8,128)(2,1)}, bf16[384,128]{1,0:T(8,128)(2,1)}, bf16[384,128]{1,0:T(8,128)(2,1)}, bf16[384,128]{1,0:T(8,128)(2,1)}) conditional(s32[]{:T(128)} %clamp.8, bf16[384,128]{1,0:T(8,128)(2,1)S(1)} %get-tuple-element.508.field_in, ...), branch_computations={%region_2.0_spmd, %region_3.0_spmd, %region_4.0_spmd, %region_5.0_... | conditional | bytes 1573056 | solution.py:49
  16.8 1.4 collective-permute-start.6
  18.2 1.3 collective-permute-start.7
  19.5 4.5 %collective-permute-start.8 = (bf16[384,128]{1,0:T(8,128)(2,1)S(1)}, bf16[384,128]{1,0:T(8,128)(2,1)}, u32[]{:S(2)}, u32[]{:S(2)}) collective-permute-start(bf16[384,128]{1,0:T(8,128)(2,1)S(1)} %param.2), channel_id=1, source_target_pairs={{16,0},{24,8},{32,16},{40,24},{48,32},{56,40},{64,48},{72,56},{80,... | collective-permute-start | bytes 294920 | tf_op jit(solution)/shard_map/while/body/eval_jaxpr/cond/branch_2_fun/ppermute | solution.py:23
  24.0 1.8 %collective-permute-start.9 = (bf16[384,128]{1,0:T(8,128)(2,1)S(1)}, bf16[384,128]{1,0:T(8,128)(2,1)}, u32[]{:S(2)}, u32[]{:S(2)}) collective-permute-start(bf16[384,128]{1,0:T(8,128)(2,1)S(1)} %param.2), channel_id=1, source_target_pairs={{24,0},{32,8},{40,16},{48,24},{56,32},{64,40},{72,48},{80,56},{88,... | collective-permute-start | bytes 294920 | tf_op jit(solution)/shard_map/while/body/eval_jaxpr/cond/branch_2_fun/ppermute | solution.py:23
  25.8 2.3 %collective-permute-done.7 = bf16[384,128]{1,0:T(8,128)(2,1)} collective-permute-done((bf16[384,128]{1,0:T(8,128)(2,1)S(1)}, bf16[384,128]{1,0:T(8,128)(2,1)}, u32[]{:S(2)}, u32[]{:S(2)}) %collective-permute-start.7) | collective-permute-done | bytes 98336 | tf_op jit(solution)/shard_map/while/body/eval_jaxpr/cond/branch_2_fun/ppermute | solution.py:23
  28.1 0.4 collective-permute-done.9
  28.5 4.4 %stage.5 = (bf16[384,128]{1,0:T(8,128)(2,1)S(1)}, f32[384,128]{1,0:T(8,128)S(1)}, bf16[3,384,128]{2,1,0:T(8,128)(2,1)S(1)}, bf16[3,384,128]{2,1,0:T(8,128)(2,1)S...) custom-call(s32[1]{0:T(128)} %bitcast.17.stage_ref, ...), custom_call_target="tpu_custom_call", output_to_operand_aliasing={{0}: (10, {}), {1}: (11, {}), {2}: (12, {}), {3}: (13, {}),... | custom-call | tf_op jit(solution)/shard_map/while/body/eval_jaxpr/stage/pallas_call | solution.py:390
  34.8 11.3 %conditional.2 = (bf16[384,128]{1,0:T(8,128)(2,1)}, bf16[384,128]{1,0:T(8,128)(2,1)}, bf16[384,128]{1,0:T(8,128)(2,1)}, bf16[384,128]{1,0:T(8,128)(2,1)}) conditional(s32[]{:T(128)} %clamp.8, bf16[384,128]{1,0:T(8,128)(2,1)S(1)} %get-tuple-element.508.field_in, ...), branch_computations={%region_2.0_spmd, %region_3.0_spmd, %region_4.0_spmd, %region_5.0_... | conditional | bytes 1573056 | solution.py:49
  34.8 1.4 collective-permute-start.10
  36.2 2.2 %collective-permute-start.11 = (bf16[384,128]{1,0:T(8,128)(2,1)S(1)}, bf16[384,128]{1,0:T(8,128)(2,1)}, u32[]{:S(2)}, u32[]{:S(2)}) collective-permute-start(bf16[384,128]{1,0:T(8,128)(2,1)S(1)} %param.3), channel_id=1, source_target_pairs={{232,0},{240,8},{248,16},{0,24},{8,32},{16,40},{24,48},{32,56},{40... | collective-permute-start | bytes 294920 | tf_op jit(solution)/shard_map/while/body/eval_jaxpr/cond/branch_3_fun/ppermute | solution.py:23
  38.4 1.7 %collective-permute-start.12 = (bf16[384,128]{1,0:T(8,128)(2,1)S(1)}, bf16[384,128]{1,0:T(8,128)(2,1)}, u32[]{:S(2)}, u32[]{:S(2)}) collective-permute-start(bf16[384,128]{1,0:T(8,128)(2,1)S(1)} %param.3), channel_id=1, source_target_pairs={{24,0},{32,8},{40,16},{48,24},{56,32},{64,40},{72,48},{80,56},{88,... | collective-permute-start | bytes 294920 | tf_op jit(solution)/shard_map/while/body/eval_jaxpr/cond/branch_3_fun/ppermute | solution.py:23
  40.0 1.4 collective-permute-start.13
  41.5 2.4 %collective-permute-done.11 = bf16[384,128]{1,0:T(8,128)(2,1)} collective-permute-done((bf16[384,128]{1,0:T(8,128)(2,1)S(1)}, bf16[384,128]{1,0:T(8,128)(2,1)}, u32[]{:S(2)}, u32[]{:S(2)}) %collective-permute-start.11) | collective-permute-done | bytes 98336 | tf_op jit(solution)/shard_map/while/body/eval_jaxpr/cond/branch_3_fun/ppermute | solution.py:23
  43.9 2.1 %collective-permute-done.13 = bf16[384,128]{1,0:T(8,128)(2,1)} collective-permute-done((bf16[384,128]{1,0:T(8,128)(2,1)S(1)}, bf16[384,128]{1,0:T(8,128)(2,1)}, u32[]{:S(2)}, u32[]{:S(2)}) %collective-permute-start.13) | collective-permute-done | bytes 98336 | tf_op jit(solution)/shard_map/while/body/eval_jaxpr/cond/branch_3_fun/ppermute | solution.py:23
  46.0 6.4 %stage.5 = (bf16[384,128]{1,0:T(8,128)(2,1)S(1)}, f32[384,128]{1,0:T(8,128)S(1)}, bf16[3,384,128]{2,1,0:T(8,128)(2,1)S(1)}, bf16[3,384,128]{2,1,0:T(8,128)(2,1)S...) custom-call(s32[1]{0:T(128)} %bitcast.17.stage_ref, ...), custom_call_target="tpu_custom_call", output_to_operand_aliasing={{0}: (10, {}), {1}: (11, {}), {2}: (12, {}), {3}: (13, {}),... | custom-call | tf_op jit(solution)/shard_map/while/body/eval_jaxpr/stage/pallas_call | solution.py:390
  54.3 11.6 %conditional.2 = (bf16[384,128]{1,0:T(8,128)(2,1)}, bf16[384,128]{1,0:T(8,128)(2,1)}, bf16[384,128]{1,0:T(8,128)(2,1)}, bf16[384,128]{1,0:T(8,128)(2,1)}) conditional(s32[]{:T(128)} %clamp.8, bf16[384,128]{1,0:T(8,128)(2,1)S(1)} %get-tuple-element.508.field_in, ...), branch_computations={%region_2.0_spmd, %region_3.0_spmd, %region_4.0_spmd, %region_5.0_... | conditional | bytes 1573056 | solution.py:49
  54.3 2.9 %collective-permute-start.10 = (bf16[384,128]{1,0:T(8,128)(2,1)S(1)}, bf16[384,128]{1,0:T(8,128)(2,1)}, u32[]{:S(2)}, u32[]{:S(2)}) collective-permute-start(bf16[384,128]{1,0:T(8,128)(2,1)S(1)} %param.3), channel_id=1, source_target_pairs={{224,0},{232,8},{240,16},{248,24},{0,32},{8,40},{16,48},{24,56},{3... | collective-permute-start | bytes 294920 | tf_op jit(solution)/shard_map/while/body/eval_jaxpr/cond/branch_3_fun/ppermute | solution.py:23
  57.2 1.6 %collective-permute-start.11 = (bf16[384,128]{1,0:T(8,128)(2,1)S(1)}, bf16[384,128]{1,0:T(8,128)(2,1)}, u32[]{:S(2)}, u32[]{:S(2)}) collective-permute-start(bf16[384,128]{1,0:T(8,128)(2,1)S(1)} %param.3), channel_id=1, source_target_pairs={{232,0},{240,8},{248,16},{0,24},{8,32},{16,40},{24,48},{32,56},{40... | collective-permute-start | bytes 294920 | tf_op jit(solution)/shard_map/while/body/eval_jaxpr/cond/branch_3_fun/ppermute | solution.py:23
  58.8 2.3 %collective-permute-start.12 = (bf16[384,128]{1,0:T(8,128)(2,1)S(1)}, bf16[384,128]{1,0:T(8,128)(2,1)}, u32[]{:S(2)}, u32[]{:S(2)}) collective-permute-start(bf16[384,128]{1,0:T(8,128)(2,1)S(1)} %param.3), channel_id=1, source_target_pairs={{24,0},{32,8},{40,16},{48,24},{56,32},{64,40},{72,48},{80,56},{88,... | collective-permute-start | bytes 294920 | tf_op jit(solution)/shard_map/while/body/eval_jaxpr/cond/branch_3_fun/ppermute | solution.py:23
  61.1 2.5 %collective-permute-done.11 = bf16[384,128]{1,0:T(8,128)(2,1)} collective-permute-done((bf16[384,128]{1,0:T(8,128)(2,1)S(1)}, bf16[384,128]{1,0:T(8,128)(2,1)}, u32[]{:S(2)}, u32[]{:S(2)}) %collective-permute-start.11) | collective-permute-done | bytes 98336 | tf_op jit(solution)/shard_map/while/body/eval_jaxpr/cond/branch_3_fun/ppermute | solution.py:23
  63.6 0.1 collective-permute-done.12
  63.7 2.2 %collective-permute-done.13 = bf16[384,128]{1,0:T(8,128)(2,1)} collective-permute-done((bf16[384,128]{1,0:T(8,128)(2,1)S(1)}, bf16[384,128]{1,0:T(8,128)(2,1)}, u32[]{:S(2)}, u32[]{:S(2)}) %collective-permute-start.13) | collective-permute-done | bytes 98336 | tf_op jit(solution)/shard_map/while/body/eval_jaxpr/cond/branch_3_fun/ppermute | solution.py:23
  65.9 4.2 %stage.5 = (bf16[384,128]{1,0:T(8,128)(2,1)S(1)}, f32[384,128]{1,0:T(8,128)S(1)}, bf16[3,384,128]{2,1,0:T(8,128)(2,1)S(1)}, bf16[3,384,128]{2,1,0:T(8,128)(2,1)S...) custom-call(s32[1]{0:T(128)} %bitcast.17.stage_ref, ...), custom_call_target="tpu_custom_call", output_to_operand_aliasing={{0}: (10, {}), {1}: (11, {}), {2}: (12, {}), {3}: (13, {}),... | custom-call | tf_op jit(solution)/shard_map/while/body/eval_jaxpr/stage/pallas_call | solution.py:390
  72.0 9.8 %conditional.2 = (bf16[384,128]{1,0:T(8,128)(2,1)}, bf16[384,128]{1,0:T(8,128)(2,1)}, bf16[384,128]{1,0:T(8,128)(2,1)}, bf16[384,128]{1,0:T(8,128)(2,1)}) conditional(s32[]{:T(128)} %clamp.8, bf16[384,128]{1,0:T(8,128)(2,1)S(1)} %get-tuple-element.508.field_in, ...), branch_computations={%region_2.0_spmd, %region_3.0_spmd, %region_4.0_spmd, %region_5.0_... | conditional | bytes 1573056 | solution.py:49
  72.0 1.7 %collective-permute-start.6 = (bf16[384,128]{1,0:T(8,128)(2,1)S(1)}, bf16[384,128]{1,0:T(8,128)(2,1)}, u32[]{:S(2)}, u32[]{:S(2)}) collective-permute-start(bf16[384,128]{1,0:T(8,128)(2,1)S(1)} %param.2), channel_id=1, source_target_pairs={{232,0},{240,8},{248,16},{0,24},{8,32},{16,40},{24,48},{32,56},{40... | collective-permute-start | bytes 294920 | tf_op jit(solution)/shard_map/while/body/eval_jaxpr/cond/branch_2_fun/ppermute | solution.py:23
  73.7 3.6 %collective-permute-start.8 = (bf16[384,128]{1,0:T(8,128)(2,1)S(1)}, bf16[384,128]{1,0:T(8,128)(2,1)}, u32[]{:S(2)}, u32[]{:S(2)}) collective-permute-start(bf16[384,128]{1,0:T(8,128)(2,1)S(1)} %param.2), channel_id=1, source_target_pairs={{16,0},{24,8},{32,16},{40,24},{48,32},{56,40},{64,48},{72,56},{80,... | collective-permute-start | bytes 294920 | tf_op jit(solution)/shard_map/while/body/eval_jaxpr/cond/branch_2_fun/ppermute | solution.py:23
  77.3 0.7 collective-permute-start.9
  78.0 0.5 collective-permute-done.6
  78.4 2.3 %collective-permute-done.7 = bf16[384,128]{1,0:T(8,128)(2,1)} collective-permute-done((bf16[384,128]{1,0:T(8,128)(2,1)S(1)}, bf16[384,128]{1,0:T(8,128)(2,1)}, u32[]{:S(2)}, u32[]{:S(2)}) %collective-permute-start.7) | collective-permute-done | bytes 98336 | tf_op jit(solution)/shard_map/while/body/eval_jaxpr/cond/branch_2_fun/ppermute | solution.py:23
  80.7 1.0 collective-permute-done.9
  81.8 4.2 %stage.5 = (bf16[384,128]{1,0:T(8,128)(2,1)S(1)}, f32[384,128]{1,0:T(8,128)S(1)}, bf16[3,384,128]{2,1,0:T(8,128)(2,1)S(1)}, bf16[3,384,128]{2,1,0:T(8,128)(2,1)S...) custom-call(s32[1]{0:T(128)} %bitcast.17.stage_ref, ...), custom_call_target="tpu_custom_call", output_to_operand_aliasing={{0}: (10, {}), {1}: (11, {}), {2}: (12, {}), {3}: (13, {}),... | custom-call | tf_op jit(solution)/shard_map/while/body/eval_jaxpr/stage/pallas_call | solution.py:390
  87.8 4.7 %conditional.2 = (bf16[384,128]{1,0:T(8,128)(2,1)}, bf16[384,128]{1,0:T(8,128)(2,1)}, bf16[384,128]{1,0:T(8,128)(2,1)}, bf16[384,128]{1,0:T(8,128)(2,1)}) conditional(s32[]{:T(128)} %clamp.8, bf16[384,128]{1,0:T(8,128)(2,1)S(1)} %get-tuple-element.508.field_in, ...), branch_computations={%region_2.0_spmd, %region_3.0_spmd, %region_4.0_spmd, %region_5.0_... | conditional | bytes 1573056 | solution.py:49
  87.8 0.5 collective-permute-start
  88.4 1.1 collective-permute-start.1
  89.5 0.6 copy.27
  90.1 0.6 copy.28
  90.8 1.7 %collective-permute-done.1 = bf16[384,128]{1,0:T(8,128)(2,1)} collective-permute-done((bf16[384,128]{1,0:T(8,128)(2,1)S(1)}, bf16[384,128]{1,0:T(8,128)(2,1)}, u32[]{:S(2)}, u32[]{:S(2)}) %collective-permute-start.1) | collective-permute-done | bytes 98336 | tf_op jit(solution)/shard_map/while/body/eval_jaxpr/cond/branch_0_fun/ppermute | solution.py:23
  92.5 3.5 %stage.5 = (bf16[384,128]{1,0:T(8,128)(2,1)S(1)}, f32[384,128]{1,0:T(8,128)S(1)}, bf16[3,384,128]{2,1,0:T(8,128)(2,1)S(1)}, bf16[3,384,128]{2,1,0:T(8,128)(2,1)S...) custom-call(s32[1]{0:T(128)} %bitcast.17.stage_ref, ...), custom_call_target="tpu_custom_call", output_to_operand_aliasing={{0}: (10, {}), {1}: (11, {}), {2}: (12, {}), {3}: (13, {}),... | custom-call | tf_op jit(solution)/shard_map/while/body/eval_jaxpr/stage/pallas_call | solution.py:390
  97.2 7.2 %all_to_all.10 = bf16[2,1792,128]{2,1,0:T(8,128)(2,1)S(1)} all-to-all(bf16[2,1792,128]{2,1,0:T(8,128)(2,1)S(1)} %bitcast.19), channel_id=1, replica_groups=mesh['z'=8,'xl'=2,'core'=2,'mem'=8] {'core'}, dimensions={0} | all-to-all | bytes 1835008 | tf_op jit(solution)/shard_map/all_to_all | solution.py:295
  104.4 0.4 reduce_sum.34
  104.9 16.8 %all_to_all.11 = bf16[8,224,128]{2,1,0:T(8,128)(2,1)S(1)} all-to-all(bf16[8,224,128]{2,1,0:T(8,128)(2,1)S(1)} %bitcast.21), channel_id=1, replica_groups=mesh['z'=8,'xl'=2,'core'=2,'mem'=8] {'mem'}, dimensions={0} | all-to-all | bytes 917504 | tf_op jit(solution)/shard_map/all_to_all | solution.py:297
  121.7 0.1 collective-permute-start.14
  121.8 3.0 %collective-permute-done.14 = bf16[224,128]{1,0:T(8,128)(2,1)S(1)} collective-permute-done((bf16[224,128]{1,0:T(8,128)(2,1)S(1)}, bf16[224,128]{1,0:T(8,128)(2,1)S(1)}, u32[]{:S(2)}, u32[]{:S(2)}) %collective-permute-start.14) | collective-permute-done | bytes 57376 | tf_op jit(solution)/shard_map/ppermute | solution.py:303
  124.8 0.1 collective-permute-start.15
  124.9 3.0 %collective-permute-done.15 = bf16[224,128]{1,0:T(8,128)(2,1)S(1)} collective-permute-done((bf16[224,128]{1,0:T(8,128)(2,1)S(1)}, bf16[224,128]{1,0:T(8,128)(2,1)S(1)}, u32[]{:S(2)}, u32[]{:S(2)}) %collective-permute-start.15) | collective-permute-done | bytes 57376 | tf_op jit(solution)/shard_map/ppermute | solution.py:303
  128.0 0.1 collective-permute-start.16
  128.1 4.2 %collective-permute-done.16 = bf16[224,128]{1,0:T(8,128)(2,1)S(1)} collective-permute-done((bf16[224,128]{1,0:T(8,128)(2,1)S(1)}, bf16[224,128]{1,0:T(8,128)(2,1)S(1)}, u32[]{:S(2)}, u32[]{:S(2)}) %collective-permute-start.16) | collective-permute-done | bytes 57376 | tf_op jit(solution)/shard_map/ppermute | solution.py:303
  132.4 1.8 %collective-permute-start.17 = (bf16[224,128]{1,0:T(8,128)(2,1)S(1)}, bf16[224,128]{1,0:T(8,128)(2,1)S(1)}, u32[]{:S(2)}, u32[]{:S(2)}) collective-permute-start(bf16[224,128]{1,0:T(8,128)(2,1)S(1)} %add_convert_fusion.1), channel_id=1, source_target_pairs={{0,224},{32,192},{64,160},{96,128},{128,96},{160,64},{192,32},{224... | collective-permute-start | bytes 172040 | tf_op jit(solution)/shard_map/ppermute | solution.py:303
  134.1 0.7 copy_bitcast_fusion
  134.9 2.4 %collective-permute-done.17 = bf16[224,128]{1,0:T(8,128)(2,1)S(1)} collective-permute-done((bf16[224,128]{1,0:T(8,128)(2,1)S(1)}, bf16[224,128]{1,0:T(8,128)(2,1)S(1)}, u32[]{:S(2)}, u32[]{:S(2)}) %collective-permute-start.17) | collective-permute-done | bytes 57376 | tf_op jit(solution)/shard_map/ppermute | solution.py:303
  137.3 7.8 %all-gather = bf16[448,128]{1,0:T(8,128)(2,1)S(1)} all-gather(bf16[224,128]{1,0:T(8,128)(2,1)S(1)} %add_convert_fusion), channel_id=2, replica_groups=mesh['z'=8,'xl'=2,'core'=2,'mem'=8] {'core'}, dimensions={0}, use_global_device_ids=true | all-gather | bytes 172032 | tf_op jit(solution)/shard_map/all_gather | solution.py:305
  145.2 0.7 convert_multiply_fusion
  (32 shorter events, 0.2 us)
Async XLA Ops:
  0.6 0.7 copy-start.3
  2.9 7.5 %copy-start = (bf16[3,128,512]{2,1,0:T(8,128)(2,1)S(1)}, bf16[3,128,512]{2,1,0:T(8,128)(2,1)}, u32[]{:S(2)}) copy-start(bf16[3,128,512]{2,1,0:T(8,128)(2,1)} %get-tuple-element.543.entries) | copy-start | bytes 1179652 | tf_op jit(solution)/shard_map/while
  3.7 4.7 %collective-permute-start = (bf16[384,128]{1,0:T(8,128)(2,1)S(1)}, bf16[384,128]{1,0:T(8,128)(2,1)}, u32[]{:S(2)}, u32[]{:S(2)}) collective-permute-start(bf16[384,128]{1,0:T(8,128)(2,1)S(1)} %param), channel_id=1, source_target_pairs={{248,0},{0,8},{8,16},{16,24},{24,32},{32,40},{40,48},{48,56},{56,6... | collective-permute-start | bytes 294920 | tf_op jit(solution)/shard_map/while/body/eval_jaxpr/cond/branch_0_fun/ppermute | solution.py:23
  6.3 4.1 %collective-permute-start.1 = (bf16[384,128]{1,0:T(8,128)(2,1)S(1)}, bf16[384,128]{1,0:T(8,128)(2,1)}, u32[]{:S(2)}, u32[]{:S(2)}) collective-permute-start(bf16[384,128]{1,0:T(8,128)(2,1)S(1)} %param), channel_id=1, source_target_pairs={{8,0},{16,8},{24,16},{32,24},{40,32},{48,40},{56,48},{64,56},{72,6... | collective-permute-start | bytes 294920 | tf_op jit(solution)/shard_map/while/body/eval_jaxpr/cond/branch_0_fun/ppermute | solution.py:23
  16.0 12.4 %copy-start = (bf16[3,128,512]{2,1,0:T(8,128)(2,1)S(1)}, bf16[3,128,512]{2,1,0:T(8,128)(2,1)}, u32[]{:S(2)}) copy-start(bf16[3,128,512]{2,1,0:T(8,128)(2,1)} %get-tuple-element.543.entries) | copy-start | bytes 1179652 | tf_op jit(solution)/shard_map/while
  16.8 9.0 %collective-permute-start.6 = (bf16[384,128]{1,0:T(8,128)(2,1)S(1)}, bf16[384,128]{1,0:T(8,128)(2,1)}, u32[]{:S(2)}, u32[]{:S(2)}) collective-permute-start(bf16[384,128]{1,0:T(8,128)(2,1)S(1)} %param.2), channel_id=1, source_target_pairs={{232,0},{240,8},{248,16},{0,24},{8,32},{16,40},{24,48},{32,56},{40... | collective-permute-start | bytes 294920 | tf_op jit(solution)/shard_map/while/body/eval_jaxpr/cond/branch_2_fun/ppermute | solution.py:23
  18.2 9.9 %collective-permute-start.7 = (bf16[384,128]{1,0:T(8,128)(2,1)S(1)}, bf16[384,128]{1,0:T(8,128)(2,1)}, u32[]{:S(2)}, u32[]{:S(2)}) collective-permute-start(bf16[384,128]{1,0:T(8,128)(2,1)S(1)} %param.2), channel_id=1, source_target_pairs={{240,0},{248,8},{0,16},{8,24},{16,32},{24,40},{32,48},{40,56},{48,... | collective-permute-start | bytes 294920 | tf_op jit(solution)/shard_map/while/body/eval_jaxpr/cond/branch_2_fun/ppermute | solution.py:23
  19.5 8.7 %collective-permute-start.8 = (bf16[384,128]{1,0:T(8,128)(2,1)S(1)}, bf16[384,128]{1,0:T(8,128)(2,1)}, u32[]{:S(2)}, u32[]{:S(2)}) collective-permute-start(bf16[384,128]{1,0:T(8,128)(2,1)S(1)} %param.2), channel_id=1, source_target_pairs={{16,0},{24,8},{32,16},{40,24},{48,32},{56,40},{64,48},{72,56},{80,... | collective-permute-start | bytes 294920 | tf_op jit(solution)/shard_map/while/body/eval_jaxpr/cond/branch_2_fun/ppermute | solution.py:23
  24.0 4.5 %collective-permute-start.9 = (bf16[384,128]{1,0:T(8,128)(2,1)S(1)}, bf16[384,128]{1,0:T(8,128)(2,1)}, u32[]{:S(2)}, u32[]{:S(2)}) collective-permute-start(bf16[384,128]{1,0:T(8,128)(2,1)S(1)} %param.2), channel_id=1, source_target_pairs={{24,0},{32,8},{40,16},{48,24},{56,32},{64,40},{72,48},{80,56},{88,... | collective-permute-start | bytes 294920 | tf_op jit(solution)/shard_map/while/body/eval_jaxpr/cond/branch_2_fun/ppermute | solution.py:23
  34.1 12.0 %copy-start = (bf16[3,128,512]{2,1,0:T(8,128)(2,1)S(1)}, bf16[3,128,512]{2,1,0:T(8,128)(2,1)}, u32[]{:S(2)}) copy-start(bf16[3,128,512]{2,1,0:T(8,128)(2,1)} %get-tuple-element.543.entries) | copy-start | bytes 1179652 | tf_op jit(solution)/shard_map/while
  34.8 6.7 %collective-permute-start.10 = (bf16[384,128]{1,0:T(8,128)(2,1)S(1)}, bf16[384,128]{1,0:T(8,128)(2,1)}, u32[]{:S(2)}, u32[]{:S(2)}) collective-permute-start(bf16[384,128]{1,0:T(8,128)(2,1)S(1)} %param.3), channel_id=1, source_target_pairs={{224,0},{232,8},{240,16},{248,24},{0,32},{8,40},{16,48},{24,56},{3... | collective-permute-start | bytes 294920 | tf_op jit(solution)/shard_map/while/body/eval_jaxpr/cond/branch_3_fun/ppermute | solution.py:23
  36.2 7.7 %collective-permute-start.11 = (bf16[384,128]{1,0:T(8,128)(2,1)S(1)}, bf16[384,128]{1,0:T(8,128)(2,1)}, u32[]{:S(2)}, u32[]{:S(2)}) collective-permute-start(bf16[384,128]{1,0:T(8,128)(2,1)S(1)} %param.3), channel_id=1, source_target_pairs={{232,0},{240,8},{248,16},{0,24},{8,32},{16,40},{24,48},{32,56},{40... | collective-permute-start | bytes 294920 | tf_op jit(solution)/shard_map/while/body/eval_jaxpr/cond/branch_3_fun/ppermute | solution.py:23
  38.4 5.5 %collective-permute-start.12 = (bf16[384,128]{1,0:T(8,128)(2,1)S(1)}, bf16[384,128]{1,0:T(8,128)(2,1)}, u32[]{:S(2)}, u32[]{:S(2)}) collective-permute-start(bf16[384,128]{1,0:T(8,128)(2,1)S(1)} %param.3), channel_id=1, source_target_pairs={{24,0},{32,8},{40,16},{48,24},{56,32},{64,40},{72,48},{80,56},{88,... | collective-permute-start | bytes 294920 | tf_op jit(solution)/shard_map/while/body/eval_jaxpr/cond/branch_3_fun/ppermute | solution.py:23
  40.0 6.0 %collective-permute-start.13 = (bf16[384,128]{1,0:T(8,128)(2,1)S(1)}, bf16[384,128]{1,0:T(8,128)(2,1)}, u32[]{:S(2)}, u32[]{:S(2)}) collective-permute-start(bf16[384,128]{1,0:T(8,128)(2,1)S(1)} %param.3), channel_id=1, source_target_pairs={{32,0},{40,8},{48,16},{56,24},{64,32},{72,40},{80,48},{88,56},{96,... | collective-permute-start | bytes 294920 | tf_op jit(solution)/shard_map/while/body/eval_jaxpr/cond/branch_3_fun/ppermute | solution.py:23
  53.6 12.3 %copy-start = (bf16[3,128,512]{2,1,0:T(8,128)(2,1)S(1)}, bf16[3,128,512]{2,1,0:T(8,128)(2,1)}, u32[]{:S(2)}) copy-start(bf16[3,128,512]{2,1,0:T(8,128)(2,1)} %get-tuple-element.543.entries) | copy-start | bytes 1179652 | tf_op jit(solution)/shard_map/while
  54.3 6.8 %collective-permute-start.10 = (bf16[384,128]{1,0:T(8,128)(2,1)S(1)}, bf16[384,128]{1,0:T(8,128)(2,1)}, u32[]{:S(2)}, u32[]{:S(2)}) collective-permute-start(bf16[384,128]{1,0:T(8,128)(2,1)S(1)} %param.3), channel_id=1, source_target_pairs={{224,0},{232,8},{240,16},{248,24},{0,32},{8,40},{16,48},{24,56},{3... | collective-permute-start | bytes 294920 | tf_op jit(solution)/shard_map/while/body/eval_jaxpr/cond/branch_3_fun/ppermute | solution.py:23
  57.2 6.4 %collective-permute-start.11 = (bf16[384,128]{1,0:T(8,128)(2,1)S(1)}, bf16[384,128]{1,0:T(8,128)(2,1)}, u32[]{:S(2)}, u32[]{:S(2)}) collective-permute-start(bf16[384,128]{1,0:T(8,128)(2,1)S(1)} %param.3), channel_id=1, source_target_pairs={{232,0},{240,8},{248,16},{0,24},{8,32},{16,40},{24,48},{32,56},{40... | collective-permute-start | bytes 294920 | tf_op jit(solution)/shard_map/while/body/eval_jaxpr/cond/branch_3_fun/ppermute | solution.py:23
  58.8 4.9 %collective-permute-start.12 = (bf16[384,128]{1,0:T(8,128)(2,1)S(1)}, bf16[384,128]{1,0:T(8,128)(2,1)}, u32[]{:S(2)}, u32[]{:S(2)}) collective-permute-start(bf16[384,128]{1,0:T(8,128)(2,1)S(1)} %param.3), channel_id=1, source_target_pairs={{24,0},{32,8},{40,16},{48,24},{56,32},{64,40},{72,48},{80,56},{88,... | collective-permute-start | bytes 294920 | tf_op jit(solution)/shard_map/while/body/eval_jaxpr/cond/branch_3_fun/ppermute | solution.py:23
  61.1 4.8 %collective-permute-start.13 = (bf16[384,128]{1,0:T(8,128)(2,1)S(1)}, bf16[384,128]{1,0:T(8,128)(2,1)}, u32[]{:S(2)}, u32[]{:S(2)}) collective-permute-start(bf16[384,128]{1,0:T(8,128)(2,1)S(1)} %param.3), channel_id=1, source_target_pairs={{32,0},{40,8},{48,16},{56,24},{64,32},{72,40},{80,48},{88,56},{96,... | collective-permute-start | bytes 294920 | tf_op jit(solution)/shard_map/while/body/eval_jaxpr/cond/branch_3_fun/ppermute | solution.py:23
  71.3 10.5 %copy-start = (bf16[3,128,512]{2,1,0:T(8,128)(2,1)S(1)}, bf16[3,128,512]{2,1,0:T(8,128)(2,1)}, u32[]{:S(2)}) copy-start(bf16[3,128,512]{2,1,0:T(8,128)(2,1)} %get-tuple-element.543.entries) | copy-start | bytes 1179652 | tf_op jit(solution)/shard_map/while
  72.0 6.4 %collective-permute-start.6 = (bf16[384,128]{1,0:T(8,128)(2,1)S(1)}, bf16[384,128]{1,0:T(8,128)(2,1)}, u32[]{:S(2)}, u32[]{:S(2)}) collective-permute-start(bf16[384,128]{1,0:T(8,128)(2,1)S(1)} %param.2), channel_id=1, source_target_pairs={{232,0},{240,8},{248,16},{0,24},{8,32},{16,40},{24,48},{32,56},{40... | collective-permute-start | bytes 294920 | tf_op jit(solution)/shard_map/while/body/eval_jaxpr/cond/branch_2_fun/ppermute | solution.py:23
  73.7 7.0 %collective-permute-start.7 = (bf16[384,128]{1,0:T(8,128)(2,1)S(1)}, bf16[384,128]{1,0:T(8,128)(2,1)}, u32[]{:S(2)}, u32[]{:S(2)}) collective-permute-start(bf16[384,128]{1,0:T(8,128)(2,1)S(1)} %param.2), channel_id=1, source_target_pairs={{240,0},{248,8},{0,16},{8,24},{16,32},{24,40},{32,48},{40,56},{48,... | collective-permute-start | bytes 294920 | tf_op jit(solution)/shard_map/while/body/eval_jaxpr/cond/branch_2_fun/ppermute | solution.py:23
  73.7 7.0 %collective-permute-start.8 = (bf16[384,128]{1,0:T(8,128)(2,1)S(1)}, bf16[384,128]{1,0:T(8,128)(2,1)}, u32[]{:S(2)}, u32[]{:S(2)}) collective-permute-start(bf16[384,128]{1,0:T(8,128)(2,1)S(1)} %param.2), channel_id=1, source_target_pairs={{16,0},{24,8},{32,16},{40,24},{48,32},{56,40},{64,48},{72,56},{80,... | collective-permute-start | bytes 294920 | tf_op jit(solution)/shard_map/while/body/eval_jaxpr/cond/branch_2_fun/ppermute | solution.py:23
  77.3 4.5 %collective-permute-start.9 = (bf16[384,128]{1,0:T(8,128)(2,1)S(1)}, bf16[384,128]{1,0:T(8,128)(2,1)}, u32[]{:S(2)}, u32[]{:S(2)}) collective-permute-start(bf16[384,128]{1,0:T(8,128)(2,1)S(1)} %param.2), channel_id=1, source_target_pairs={{24,0},{32,8},{40,16},{48,24},{56,32},{64,40},{72,48},{80,56},{88,... | collective-permute-start | bytes 294920 | tf_op jit(solution)/shard_map/while/body/eval_jaxpr/cond/branch_2_fun/ppermute | solution.py:23
  87.1 5.4 %copy-start = (bf16[3,128,512]{2,1,0:T(8,128)(2,1)S(1)}, bf16[3,128,512]{2,1,0:T(8,128)(2,1)}, u32[]{:S(2)}) copy-start(bf16[3,128,512]{2,1,0:T(8,128)(2,1)} %get-tuple-element.543.entries) | copy-start | bytes 1179652 | tf_op jit(solution)/shard_map/while
  87.8 3.0 %collective-permute-start = (bf16[384,128]{1,0:T(8,128)(2,1)S(1)}, bf16[384,128]{1,0:T(8,128)(2,1)}, u32[]{:S(2)}, u32[]{:S(2)}) collective-permute-start(bf16[384,128]{1,0:T(8,128)(2,1)S(1)} %param), channel_id=1, source_target_pairs={{248,0},{0,8},{8,16},{16,24},{24,32},{32,40},{40,48},{48,56},{56,6... | collective-permute-start | bytes 294920 | tf_op jit(solution)/shard_map/while/body/eval_jaxpr/cond/branch_0_fun/ppermute | solution.py:23
  88.4 4.1 %collective-permute-start.1 = (bf16[384,128]{1,0:T(8,128)(2,1)S(1)}, bf16[384,128]{1,0:T(8,128)(2,1)}, u32[]{:S(2)}, u32[]{:S(2)}) collective-permute-start(bf16[384,128]{1,0:T(8,128)(2,1)S(1)} %param), channel_id=1, source_target_pairs={{8,0},{16,8},{24,16},{32,24},{40,32},{48,40},{56,48},{64,56},{72,6... | collective-permute-start | bytes 294920 | tf_op jit(solution)/shard_map/while/body/eval_jaxpr/cond/branch_0_fun/ppermute | solution.py:23
  121.7 3.1 %collective-permute-start.14 = (bf16[224,128]{1,0:T(8,128)(2,1)S(1)}, bf16[224,128]{1,0:T(8,128)(2,1)S(1)}, u32[]{:S(2)}, u32[]{:S(2)}) collective-permute-start(bf16[224,128]{1,0:T(8,128)(2,1)S(1)} %reduce_sum.35), channel_id=1, source_target_pairs={{0,16},{16,0},{1,17},{17,1},{2,18},{18,2},{3,19},{19,3},{4,20},{20... | collective-permute-start | bytes 172040 | tf_op jit(solution)/shard_map/ppermute | solution.py:303
  124.8 3.1 %collective-permute-start.15 = (bf16[224,128]{1,0:T(8,128)(2,1)S(1)}, bf16[224,128]{1,0:T(8,128)(2,1)S(1)}, u32[]{:S(2)}, u32[]{:S(2)}) collective-permute-start(bf16[224,128]{1,0:T(8,128)(2,1)S(1)} %add_convert_fusion.3), channel_id=1, source_target_pairs={{0,32},{32,0},{64,96},{96,64},{128,160},{160,128},{192,224},{224,1... | collective-permute-start | bytes 172040 | tf_op jit(solution)/shard_map/ppermute | solution.py:303
  128.0 6.2 %copy-start.2 = (bf16[8,45,128]{2,1,0:T(8,128)(2,1)S(1)}, bf16[8,45,128]{2,1,0:T(8,128)(2,1)}, u32[]{:S(2)}) copy-start(bf16[8,45,128]{2,1,0:T(8,128)(2,1)} %get-tuple-element.300) | copy-start | bytes 276484
  128.0 6.2 %copy-start.1 = (bf16[8,45,128]{2,1,0:T(8,128)(2,1)S(1)}, bf16[8,45,128]{2,1,0:T(8,128)(2,1)}, u32[]{:S(2)}) copy-start(bf16[8,45,128]{2,1,0:T(8,128)(2,1)} %get-tuple-element.299) | copy-start | bytes 276484
  128.0 4.4 %collective-permute-start.16 = (bf16[224,128]{1,0:T(8,128)(2,1)S(1)}, bf16[224,128]{1,0:T(8,128)(2,1)S(1)}, u32[]{:S(2)}, u32[]{:S(2)}) collective-permute-start(bf16[224,128]{1,0:T(8,128)(2,1)S(1)} %add_convert_fusion.2), channel_id=1, source_target_pairs={{0,64},{32,96},{64,0},{96,32},{128,192},{160,224},{192,128},{224,1... | collective-permute-start | bytes 172040 | tf_op jit(solution)/shard_map/ppermute | solution.py:303
  132.4 4.9 %collective-permute-start.17 = (bf16[224,128]{1,0:T(8,128)(2,1)S(1)}, bf16[224,128]{1,0:T(8,128)(2,1)S(1)}, u32[]{:S(2)}, u32[]{:S(2)}) collective-permute-start(bf16[224,128]{1,0:T(8,128)(2,1)S(1)} %add_convert_fusion.1), channel_id=1, source_target_pairs={{0,224},{32,192},{64,160},{96,128},{128,96},{160,64},{192,32},{224... | collective-permute-start | bytes 172040 | tf_op jit(solution)/shard_map/ppermute | solution.py:303
